TPU v7x, 256 devices: a whole 4x4x8 slice. The times are simulated.
256 devices in a mesh: wide: 32 (over x, z_hi, core), narrow: 8 (over y, z_lo).
Axes of the slice: x: 4, y: 4, z: 8 (z_hi: 4, z_lo: 2; z = z_hi * 2 + z_lo), core: 2. Of those that a mesh axis runs over, the one named last changes fastest.
Arguments:
- state_real: float32 [8, 32, 4096, 128], P('narrow', 'wide'), may hold values from -6 to 6
- state_imag: float32 [8, 32, 4096, 128], P('narrow', 'wide'), may hold values from -6 to 6
- gates: float32 [3, 2, 128, 128], replicated, may hold values from -0.375 to 0.375
- gate_orders: int32 [3, 7], replicated, may hold values from 0 to 6, each once within a row
- phase_masks: int32 [8, 2], replicated, may hold values from 1 to 67108864, as said below
- phase_angles: float32 [8], replicated, may hold values from -3.140625 to 3.140625
Outputs:
- out_real: float32 [8, 32, 4096, 128], P('narrow', 'wide')
- out_imag: float32 [8, 32, 4096, 128], P('narrow', 'wide')
Inputs may be any that keep to these rules, and one draw needn't show every extreme that they name: `phase_masks`: each entry is 2**q for one qubit q of the whole index of 134217728 amplitudes; the two entries of a row differ.
All inputs are finite; a program needn't handle non-finite values.
Results may differ from a plain program's by a relative error of at most 0.0003.
Values sent between devices are 32-bit elements; how exact they have to be, the bound alone decides.
No kernel may reach another device: no remote copies, remote signals or barrier semaphores. Data moves between devices by JAX's collectives and lax.ppermute only.
A program may use at most 64 MiB of HBM per device.

v0:
```python
import jax
import jax.numpy as jnp
from jax import lax
from jax.sharding import PartitionSpec as P

precise = lax.Precision.HIGHEST


def partner(block, axis, stride):
    count = lax.axis_size(axis)
    route = []
    for low in range(count):
        high = low | 1 << stride
        if high != low and high < count:
            route += [(low, high), (high, low)]
    return lax.ppermute(block, axis, route)


def ordered_gate(gate_pair, order_row):
    count = order_row.shape[0]
    states = jnp.arange(2**count, dtype=jnp.int32)
    places = jnp.arange(count, dtype=jnp.int32)
    digits = states[:, None] >> places[None, :] & 1
    mapped = jnp.sum(digits << order_row[None, :], axis=1)
    permute = (mapped[:, None] == states[None, :]).astype(jnp.float32)
    real_gate = jnp.dot(
        jnp.dot(permute, gate_pair[0], precision=precise), permute.T, precision=precise
    )
    imag_gate = jnp.dot(
        jnp.dot(permute, gate_pair[1], precision=precise), permute.T, precision=precise
    )
    return (real_gate, imag_gate)


def mixing(gate_real, gate_imag, real_part, imag_part):
    out_real = jnp.dot(gate_real, real_part, precision=precise) - jnp.dot(
        gate_imag, imag_part, precision=precise
    )
    out_imag = jnp.dot(gate_real, imag_part, precision=precise) + jnp.dot(
        gate_imag, real_part, precision=precise
    )
    return (out_real, out_imag)


def phase_turn(real_part, imag_part, flat, phase_masks, phase_angles):
    angle_sum = jnp.zeros(real_part.shape, jnp.float32)
    for which in range(phase_masks.shape[0]):
        both = (flat & phase_masks[which, 0] != 0) & (flat & phase_masks[which, 1] != 0)
        angle_sum = angle_sum + jnp.where(both, phase_angles[which], 0.0)
    cosine = jnp.cos(angle_sum)
    sine = jnp.sin(angle_sum)
    return (real_part * cosine - imag_part * sine, real_part * sine + imag_part * cosine)


def global_exchange(real_part, imag_part, gate_real, gate_imag, devices, outward, inward):
    row_count, columns = real_part.shape
    gate_size = gate_real.shape[0]
    blocks = gate_size // devices
    stride = row_count // blocks
    moved_real, moved_imag = outward(
        (
            real_part.reshape(1, blocks, stride, columns),
            imag_part.reshape(1, blocks, stride, columns),
        )
    )
    mixed_real, mixed_imag = mixing(
        gate_real, gate_imag, moved_real.reshape(gate_size, -1), moved_imag.reshape(gate_size, -1)
    )
    back_real, back_imag = inward(
        (mixed_real.reshape(moved_real.shape), mixed_imag.reshape(moved_imag.shape))
    )
    return (back_real.reshape(row_count, columns), back_imag.reshape(row_count, columns))


def swap_half(pieces, which_bit, own_index, sender):
    real_part, imag_part = pieces
    blocks, devices, stride, columns = real_part.shape
    split_shape = (blocks, devices >> which_bit + 1, 2, 1 << which_bit, stride, columns)
    own_bit = own_index >> which_bit & 1
    split_real = real_part.reshape(split_shape)
    split_imag = imag_part.reshape(split_shape)
    outgoing = (
        lax.dynamic_slice_in_dim(split_real, 1 - own_bit, 1, 2),
        lax.dynamic_slice_in_dim(split_imag, 1 - own_bit, 1, 2),
    )
    gotten = sender(outgoing, which_bit)
    result = []
    for kept_whole, arrived in ((split_real, gotten[0]), (split_imag, gotten[1])):
        kept_half = lax.dynamic_slice_in_dim(kept_whole, own_bit, 1, 2)
        joined = jnp.where(
            own_bit == 0,
            jnp.concatenate([kept_half, arrived], axis=2),
            jnp.concatenate([arrived, kept_half], axis=2),
        )
        result.append(joined.reshape(real_part.shape))
    return (result[0], result[1])


def global_halves(real_part, imag_part, gate_real, gate_imag, devices, own_index, sender):
    row_count, columns = real_part.shape
    gate_size = gate_real.shape[0]
    blocks = gate_size // devices
    stride = row_count // blocks
    local_shape = (blocks, devices, stride // devices, columns)
    pieces = (real_part.reshape(local_shape), imag_part.reshape(local_shape))
    levels = devices.bit_length() - 1
    for which_bit in range(levels):
        pieces = swap_half(pieces, which_bit, own_index, sender)
    turned_real = (
        gate_real.reshape(devices, blocks, devices, blocks)
        .transpose(1, 0, 3, 2)
        .reshape(gate_size, gate_size)
    )
    turned_imag = (
        gate_imag.reshape(devices, blocks, devices, blocks)
        .transpose(1, 0, 3, 2)
        .reshape(gate_size, gate_size)
    )
    mixed_real, mixed_imag = mixing(
        turned_real, turned_imag, pieces[0].reshape(gate_size, -1), pieces[1].reshape(gate_size, -1)
    )
    pieces = (mixed_real.reshape(local_shape), mixed_imag.reshape(local_shape))
    for which_bit in range(levels):
        pieces = swap_half(pieces, which_bit, own_index, sender)
    return (pieces[0].reshape(row_count, columns), pieces[1].reshape(row_count, columns))


def body(state_real, state_imag, gates, gate_orders, phase_masks, phase_angles):
    real_part = state_real[0, 0]
    imag_part = state_imag[0, 0]
    row_count, columns = real_part.shape
    first_gate = ordered_gate(gates[0], gate_orders[0])
    second_gate = ordered_gate(gates[1], gate_orders[1])
    third_gate = ordered_gate(gates[2], gate_orders[2])
    new_real = jnp.dot(real_part, first_gate[0].T, precision=precise) - jnp.dot(
        imag_part, first_gate[1].T, precision=precise
    )
    new_imag = jnp.dot(imag_part, first_gate[0].T, precision=precise) + jnp.dot(
        real_part, first_gate[1].T, precision=precise
    )
    wide_count = lax.axis_size("wide")
    narrow_count = lax.axis_size("narrow")
    wide_index = lax.axis_index("wide")
    narrow_index = lax.axis_index("narrow")
    offset = (narrow_index * wide_count + wide_index) * (row_count * columns)
    flat = (
        offset
        + jnp.arange(row_count, dtype=jnp.int32)[:, None] * columns
        + jnp.arange(columns, dtype=jnp.int32)[None, :]
    )
    turned_real, turned_imag = phase_turn(new_real, new_imag, flat, phase_masks, phase_angles)
    middle_real, middle_imag = global_exchange(
        turned_real,
        turned_imag,
        second_gate[0],
        second_gate[1],
        wide_count,
        lambda pieces: (
            lax.all_to_all(pieces[0], "wide", split_axis=2, concat_axis=0, tiled=True),
            lax.all_to_all(pieces[1], "wide", split_axis=2, concat_axis=0, tiled=True),
        ),
        lambda pieces: (
            lax.all_to_all(pieces[0], "wide", split_axis=0, concat_axis=2, tiled=True),
            lax.all_to_all(pieces[1], "wide", split_axis=0, concat_axis=2, tiled=True),
        ),
    )
    final_real, final_imag = global_halves(
        middle_real,
        middle_imag,
        third_gate[0],
        third_gate[1],
        narrow_count,
        narrow_index,
        lambda pieces, which_bit: partner((pieces[0], pieces[1]), "narrow", which_bit),
    )
    return (final_real[None, None], final_imag[None, None])


def solution(mesh):
    placed = (P("narrow", "wide", None, None), P("narrow", "wide", None, None), P(), P(), P(), P())
    return jax.shard_map(
        body,
        mesh=mesh,
        in_specs=placed,
        out_specs=(P("narrow", "wide", None, None), P("narrow", "wide", None, None)),
        check_vma=False,
    )
```

profile of v0, /device:TPU:2, one launch (start us, length us, event | category | flops | bytes accessed | tf_op | source)
XLA Modules:
  0.0 564.3 jit_solution(16842037079720946697)
XLA Ops:
  15.4 30.1 %multiply_subtract_fusion = (f32[4096,128]{0,1:T(8,128)}, f32[4096,128]{0,1:T(8,128)S(1)}) fusion(f32[4096,128]{0,1:T(8,128)S(1)} %fusion.1, f32[]{:T(128)} %bitcast.34, s32[]{:T(128)} %bitcast.33, s32[]{:T(128)} %bitcast.32, f32[]{:T(128)} %bitcast.31, s32[]{:T(128)} %bitcast.30, s32[]{:T(128)} %bitcast.29, f32[]{:T(128)} %bitcast.28, s32[]{:T(128)} %bitcast.27, ...), kind=kOutput, calls=%fused_computation.39 | convolution fusion | flops 836763648 | bytes 10567776 | tf_op jit(solution)/shard_map/dot_general | solution.py:138
  45.5 26.3 %multiply_add_fusion = f32[4096,128]{0,1:T(8,128)S(1)} fusion(f32[4096,128]{0,1:T(8,128)S(1)} %get-tuple-element.54, f32[4096,128]{0,1:T(8,128)S(1)} %fusion.1, f32[]{:T(128)} %bitcast.34, s32[]{:T(128)} %bitcast.33, s32[]{:T(128)} %bitcast.32, f32[]{:T(128)} %bitcast.31, s32[]{:T(128)} %bitcast.30, s32[]{:T(128)} %bitcast.29, f32[]{:T(128)} %bitcast.28, ...), kind=kLoop, calls=%fused_computation.38 | loop fusion | flops 30932992 | bytes 6307936 | tf_op jit(solution)/shard_map/add | solution.py:52
  74.3 3.9 copy.46
  78.2 11.6 %all-to-all-start.1 = ((f32[1,4,1024,128]{3,1,0,2:T(4,128)}), f32[1,4,1024,128]{3,1,0,2:T(4,128)S(1)}, u32[]{:S(2)}, u32[]{:S(2)}) async-start(f32[1,4,1024,128]{3,1,0,2:T(4,128)} %copy.46), calls=%async_computation.1 | async-start | bytes 4194304 | tf_op jit(solution)/shard_map/all_to_all | solution.py:160
  89.8 3.6 reshape.422
  93.5 3.9 copy.43
  97.4 40.4 %all-to-all-done.1 = f32[1,4,1024,128]{3,1,0,2:T(4,128)S(1)} async-done(((f32[1,4,1024,128]{3,1,0,2:T(4,128)}), f32[1,4,1024,128]{3,1,0,2:T(4,128)S(1)}, u32[]{:S(2)}, u32[]{:S(2)}) %all-to-all-start.1) | async-done | bytes 2097184 | tf_op jit(solution)/shard_map/all_to_all | solution.py:160
  137.8 8.8 %all-to-all-start = ((f32[1,4,1024,128]{3,1,0,2:T(4,128)}), f32[1,4,1024,128]{3,1,0,2:T(4,128)}, u32[]{:S(2)}, u32[]{:S(2)}) async-start(f32[1,4,1024,128]{3,1,0,2:T(4,128)} %copy.43), calls=%async_computation | async-start | bytes 4194304 | tf_op jit(solution)/shard_map/all_to_all | solution.py:159
  148.0 41.3 %all-to-all-done = f32[1,4,1024,128]{3,1,0,2:T(4,128)} async-done(((f32[1,4,1024,128]{3,1,0,2:T(4,128)}), f32[1,4,1024,128]{3,1,0,2:T(4,128)}, u32[]{:S(2)}, u32[]{:S(2)}) %all-to-all-start) | async-done | bytes 2097184 | tf_op jit(solution)/shard_map/all_to_all | solution.py:159
  199.0 11.4 %all-to-all-start.2 = ((f32[32,4,32,128]{3,2,1,0:T(8,128)}), f32[32,4,32,128]{3,2,1,0:T(8,128)}, u32[]{:S(2)}, u32[]{:S(2)}) async-start(f32[32,4,32,128]{3,2,1,0:T(8,128)} %bitcast.200), calls=%async_computation.2 | async-start | bytes 4194304 | tf_op jit(solution)/shard_map/all_to_all | solution.py:163
  218.3 39.5 %all-to-all-done.2 = f32[32,4,32,128]{3,2,1,0:T(8,128)} async-done(((f32[32,4,32,128]{3,2,1,0:T(8,128)}), f32[32,4,32,128]{3,2,1,0:T(8,128)}, u32[]{:S(2)}, u32[]{:S(2)}) %all-to-all-start.2) | async-done | bytes 2097184 | tf_op jit(solution)/shard_map/all_to_all | solution.py:163
  257.8 9.0 %all-to-all-start.3 = ((f32[32,4,32,128]{3,2,1,0:T(8,128)}), f32[32,4,32,128]{3,2,1,0:T(8,128)}, u32[]{:S(2)}, u32[]{:S(2)}) async-start(f32[32,4,32,128]{3,2,1,0:T(8,128)} %bitcast.199), calls=%async_computation.3 | async-start | bytes 4194304 | tf_op jit(solution)/shard_map/all_to_all | solution.py:164
  270.2 3.7 collective-permute-start
  274.0 41.2 %all-to-all-done.3 = f32[32,4,32,128]{3,2,1,0:T(8,128)} async-done(((f32[32,4,32,128]{3,2,1,0:T(8,128)}), f32[32,4,32,128]{3,2,1,0:T(8,128)}, u32[]{:S(2)}, u32[]{:S(2)}) %all-to-all-start.3) | async-done | bytes 2097184 | tf_op jit(solution)/shard_map/all_to_all | solution.py:164
  321.3 16.5 %collective-permute-done = f32[16,4,1,1,32,128]{5,4,2,1,0,3:T(8,128)} collective-permute-done((f32[16,4,1,1,32,128]{5,4,2,1,0,3:T(8,128)}, f32[16,4,1,1,32,128]{5,4,2,1,0,3:T(8,128)}, u32[]{:S(2)}, u32[]{:S(2)}) %collective-permute-start) | collective-permute-done | bytes 1048608 | tf_op jit(solution)/shard_map/ppermute | solution.py:16
  343.8 16.4 %collective-permute-done.3 = f32[16,4,1,1,32,128]{5,4,2,1,0,3:T(8,128)} collective-permute-done((f32[16,4,1,1,32,128]{5,4,2,1,0,3:T(8,128)}, f32[16,4,1,1,32,128]{5,4,2,1,0,3:T(8,128)}, u32[]{:S(2)}, u32[]{:S(2)}) %collective-permute-start.3) | collective-permute-done | bytes 1048608 | tf_op jit(solution)/shard_map/ppermute | solution.py:16
  376.8 14.2 %collective-permute-done.4 = f32[16,2,1,2,32,128]{5,4,3,2,1,0:T(8,128)} collective-permute-done((f32[16,2,1,2,32,128]{5,4,3,2,1,0:T(8,128)}, f32[16,2,1,2,32,128]{5,4,3,2,1,0:T(8,128)}, u32[]{:S(2)}, u32[]{:S(2)}) %collective-permute-start.4) | collective-permute-done | bytes 1048608 | tf_op jit(solution)/shard_map/ppermute | solution.py:16
  400.8 15.2 %collective-permute-done.2 = f32[16,1,1,4,32,128]{5,4,3,2,0,1:T(8,128)} collective-permute-done((f32[16,1,1,4,32,128]{5,4,3,2,0,1:T(8,128)}, f32[16,1,1,4,32,128]{5,4,3,2,0,1:T(8,128)}, u32[]{:S(2)}, u32[]{:S(2)}) %collective-permute-start.2) | collective-permute-done | bytes 1048608 | tf_op jit(solution)/shard_map/ppermute | solution.py:16
  421.0 16.4 %collective-permute-done.5 = f32[16,1,1,4,32,128]{5,4,3,2,0,1:T(8,128)} collective-permute-done((f32[16,1,1,4,32,128]{5,4,3,2,0,1:T(8,128)}, f32[16,1,1,4,32,128]{5,4,3,2,0,1:T(8,128)}, u32[]{:S(2)}, u32[]{:S(2)}) %collective-permute-start.5) | collective-permute-done | bytes 1048608 | tf_op jit(solution)/shard_map/ppermute | solution.py:16
  452.1 20.3 %collective-permute-done.6 = f32[16,4,1,1,32,128]{5,4,2,1,0,3:T(8,128)S(1)} collective-permute-done((f32[16,4,1,1,32,128]{5,4,2,1,0,3:T(8,128)S(1)}, f32[16,4,1,1,32,128]{5,4,2,1,0,3:T(8,128)S(1)}, u32[]{:S(2)}, u32[]{:S(2)}) %collective-permute-start.6) | collective-permute-done | bytes 1048608 | tf_op jit(solution)/shard_map/ppermute | solution.py:16
  473.0 20.0 %collective-permute-done.9 = f32[16,4,1,1,32,128]{5,4,2,1,0,3:T(8,128)S(1)} collective-permute-done((f32[16,4,1,1,32,128]{5,4,2,1,0,3:T(8,128)S(1)}, f32[16,4,1,1,32,128]{5,4,2,1,0,3:T(8,128)S(1)}, u32[]{:S(2)}, u32[]{:S(2)}) %collective-permute-start.9) | collective-permute-done | bytes 1048608 | tf_op jit(solution)/shard_map/ppermute | solution.py:16
  495.8 23.8 %collective-permute-done.10 = f32[16,2,1,2,32,128]{5,4,3,2,1,0:T(8,128)S(1)} collective-permute-done((f32[16,2,1,2,32,128]{5,4,3,2,1,0:T(8,128)S(1)}, f32[16,2,1,2,32,128]{5,4,3,2,1,0:T(8,128)S(1)}, u32[]{:S(2)}, u32[]{:S(2)}) %collective-permute-start.10) | collective-permute-done | bytes 1048608 | tf_op jit(solution)/shard_map/ppermute | solution.py:16
  520.7 21.0 %collective-permute-done.8 = f32[16,1,1,4,32,128]{5,4,3,2,0,1:T(8,128)S(1)} collective-permute-done((f32[16,1,1,4,32,128]{5,4,3,2,0,1:T(8,128)S(1)}, f32[16,1,1,4,32,128]{5,4,3,2,0,1:T(8,128)S(1)}, u32[]{:S(2)}, u32[]{:S(2)}) %collective-permute-start.8) | collective-permute-done | bytes 1048608 | tf_op jit(solution)/shard_map/ppermute | solution.py:16
  543.3 18.3 %collective-permute-done.11 = f32[16,1,1,4,32,128]{5,4,3,2,0,1:T(8,128)S(1)} collective-permute-done((f32[16,1,1,4,32,128]{5,4,3,2,0,1:T(8,128)S(1)}, f32[16,1,1,4,32,128]{5,4,3,2,0,1:T(8,128)S(1)}, u32[]{:S(2)}, u32[]{:S(2)}) %collective-permute-start.11) | collective-permute-done | bytes 1048608 | tf_op jit(solution)/shard_map/ppermute | solution.py:16
  (99 shorter events, 105.7 us)
Async XLA Ops:
  0.6 10.8 %copy-start = (f32[1,1,4096,128]{3,2,1,0:T(8,128)S(1)}, f32[1,1,4096,128]{3,2,1,0:T(8,128)}, u32[]{:S(2)}) copy-start(f32[1,1,4096,128]{3,2,1,0:T(8,128)} %param.6) | copy-start | bytes 6291460
  11.4 2.0 copy-start.4
  78.2 59.5 %all-to-all-start.1 = ((f32[1,4,1024,128]{3,1,0,2:T(4,128)}), f32[1,4,1024,128]{3,1,0,2:T(4,128)S(1)}, u32[]{:S(2)}, u32[]{:S(2)}) async-start(f32[1,4,1024,128]{3,1,0,2:T(4,128)} %copy.46), calls=%async_computation.1 | async-start | bytes 4194304 | tf_op jit(solution)/shard_map/all_to_all | solution.py:160
  97.4 49.1 %copy-start.7 = (f32[3,2,128,128]{3,2,1,0:T(8,128)S(1)}, f32[3,2,128,128]{3,2,1,0:T(8,128)}, u32[]{:S(2)}) copy-start(f32[3,2,128,128]{3,2,1,0:T(8,128)} %param.8) | copy-start | bytes 1179652
  137.8 51.5 %all-to-all-start = ((f32[1,4,1024,128]{3,1,0,2:T(4,128)}), f32[1,4,1024,128]{3,1,0,2:T(4,128)}, u32[]{:S(2)}, u32[]{:S(2)}) async-start(f32[1,4,1024,128]{3,1,0,2:T(4,128)} %copy.43), calls=%async_computation | async-start | bytes 4194304 | tf_op jit(solution)/shard_map/all_to_all | solution.py:159
  191.3 3.0 copy-start.2
  199.0 58.8 %all-to-all-start.2 = ((f32[32,4,32,128]{3,2,1,0:T(8,128)}), f32[32,4,32,128]{3,2,1,0:T(8,128)}, u32[]{:S(2)}, u32[]{:S(2)}) async-start(f32[32,4,32,128]{3,2,1,0:T(8,128)} %bitcast.200), calls=%async_computation.2 | async-start | bytes 4194304 | tf_op jit(solution)/shard_map/all_to_all | solution.py:163
  210.4 3.0 copy-start.3
  257.8 57.3 %all-to-all-start.3 = ((f32[32,4,32,128]{3,2,1,0:T(8,128)}), f32[32,4,32,128]{3,2,1,0:T(8,128)}, u32[]{:S(2)}, u32[]{:S(2)}) async-start(f32[32,4,32,128]{3,2,1,0:T(8,128)} %bitcast.199), calls=%async_computation.3 | async-start | bytes 4194304 | tf_op jit(solution)/shard_map/all_to_all | solution.py:164
  270.2 67.5 %collective-permute-start = (f32[16,4,1,1,32,128]{5,4,2,1,0,3:T(8,128)}, f32[16,4,1,1,32,128]{5,4,2,1,0,3:T(8,128)}, u32[]{:S(2)}, u32[]{:S(2)}) collective-permute-start(f32[16,4,1,1,32,128]{5,4,2,1,0,3:T(8,128)} %get-tuple-element.25), channel_id=1, source_target_pairs={{0,1},{1,0},{2,3},{3,2},{4,5},{5,4},{6,7},{7,6},{8,9},{9,8},{10,11... | collective-permute-start | bytes 3145736 | tf_op jit(solution)/shard_map/ppermute | solution.py:16
  318.1 42.1 %collective-permute-start.3 = (f32[16,4,1,1,32,128]{5,4,2,1,0,3:T(8,128)}, f32[16,4,1,1,32,128]{5,4,2,1,0,3:T(8,128)}, u32[]{:S(2)}, u32[]{:S(2)}) collective-permute-start(f32[16,4,1,1,32,128]{5,4,2,1,0,3:T(8,128)} %get-tuple-element.19), channel_id=1, source_target_pairs={{0,1},{1,0},{2,3},{3,2},{4,5},{5,4},{6,7},{7,6},{8,9},{9,8},{10,11... | collective-permute-start | bytes 3145736 | tf_op jit(solution)/shard_map/ppermute | solution.py:16
  342.2 26.3 %collective-permute-start.1 = (f32[16,2,1,2,32,128]{5,4,3,2,1,0:T(8,128)}, f32[16,2,1,2,32,128]{5,4,3,2,1,0:T(8,128)}, u32[]{:S(2)}, u32[]{:S(2)}) collective-permute-start(f32[16,2,1,2,32,128]{5,4,3,2,1,0:T(8,128)} %get-tuple-element.23), channel_id=1, source_target_pairs={{0,2},{2,0},{1,3},{3,1},{4,6},{6,4},{5,7},{7,5},{8,10},{10,8},{9,1... | collective-permute-start | bytes 3145736 | tf_op jit(solution)/shard_map/ppermute | solution.py:16
  363.3 27.7 %collective-permute-start.4 = (f32[16,2,1,2,32,128]{5,4,3,2,1,0:T(8,128)}, f32[16,2,1,2,32,128]{5,4,3,2,1,0:T(8,128)}, u32[]{:S(2)}, u32[]{:S(2)}) collective-permute-start(f32[16,2,1,2,32,128]{5,4,3,2,1,0:T(8,128)} %get-tuple-element.17), channel_id=1, source_target_pairs={{0,2},{2,0},{1,3},{3,1},{4,6},{6,4},{5,7},{7,5},{8,10},{10,8},{9,1... | collective-permute-start | bytes 3145736 | tf_op jit(solution)/shard_map/ppermute | solution.py:16
  373.2 42.8 %collective-permute-start.2 = (f32[16,1,1,4,32,128]{5,4,3,2,0,1:T(8,128)}, f32[16,1,1,4,32,128]{5,4,3,2,0,1:T(8,128)}, u32[]{:S(2)}, u32[]{:S(2)}) collective-permute-start(f32[16,1,1,4,32,128]{5,4,3,2,0,1:T(8,128)} %get-tuple-element.21), channel_id=1, source_target_pairs={{0,4},{4,0},{1,5},{5,1},{2,6},{6,2},{3,7},{7,3},{8,12},{12,8},{9,1... | collective-permute-start | bytes 3145736 | tf_op jit(solution)/shard_map/ppermute | solution.py:16
  394.6 42.9 %collective-permute-start.5 = (f32[16,1,1,4,32,128]{5,4,3,2,0,1:T(8,128)}, f32[16,1,1,4,32,128]{5,4,3,2,0,1:T(8,128)}, u32[]{:S(2)}, u32[]{:S(2)}) collective-permute-start(f32[16,1,1,4,32,128]{5,4,3,2,0,1:T(8,128)} %get-tuple-element.15), channel_id=1, source_target_pairs={{0,4},{4,0},{1,5},{5,1},{2,6},{6,2},{3,7},{7,3},{8,12},{12,8},{9,1... | collective-permute-start | bytes 3145736 | tf_op jit(solution)/shard_map/ppermute | solution.py:16
  399.4 16.6 %copy-start.5 = (f32[16,1,1,4,32,128]{5,4,3,2,0,1:T(8,128)S(1)}, f32[16,1,1,4,32,128]{5,4,3,2,0,1:T(8,128)}, u32[]{:S(2)}) copy-start(f32[16,1,1,4,32,128]{5,4,3,2,0,1:T(8,128)} %get-tuple-element.20) | copy-start | bytes 3145732
  418.0 19.5 %copy-start.6 = (f32[16,1,1,4,32,128]{5,4,3,2,0,1:T(8,128)S(1)}, f32[16,1,1,4,32,128]{5,4,3,2,0,1:T(8,128)}, u32[]{:S(2)}) copy-start(f32[16,1,1,4,32,128]{5,4,3,2,0,1:T(8,128)} %get-tuple-element.14) | copy-start | bytes 3145732
  446.3 26.1 %collective-permute-start.6 = (f32[16,4,1,1,32,128]{5,4,2,1,0,3:T(8,128)S(1)}, f32[16,4,1,1,32,128]{5,4,2,1,0,3:T(8,128)S(1)}, u32[]{:S(2)}, u32[]{:S(2)}) collective-permute-start(f32[16,4,1,1,32,128]{5,4,2,1,0,3:T(8,128)S(1)} %get-tuple-element.13), channel_id=1, source_target_pairs={{0,1},{1,0},{2,3},{3,2},{4,5},{5,4},{6,7},{7,6},{8,9},{9,8},{10,11... | collective-permute-start | bytes 3145736 | tf_op jit(solution)/shard_map/ppermute | solution.py:16
  450.0 43.1 %collective-permute-start.9 = (f32[16,4,1,1,32,128]{5,4,2,1,0,3:T(8,128)S(1)}, f32[16,4,1,1,32,128]{5,4,2,1,0,3:T(8,128)S(1)}, u32[]{:S(2)}, u32[]{:S(2)}) collective-permute-start(f32[16,4,1,1,32,128]{5,4,2,1,0,3:T(8,128)S(1)} %get-tuple-element.7), channel_id=1, source_target_pairs={{0,1},{1,0},{2,3},{3,2},{4,5},{5,4},{6,7},{7,6},{8,9},{9,8},{10,11... | collective-permute-start | bytes 3145736 | tf_op jit(solution)/shard_map/ppermute | solution.py:16
  472.8 21.6 %collective-permute-start.7 = (f32[16,2,1,2,32,128]{5,4,3,2,1,0:T(8,128)S(1)}, f32[16,2,1,2,32,128]{5,4,3,2,1,0:T(8,128)S(1)}, u32[]{:S(2)}, u32[]{:S(2)}) collective-permute-start(f32[16,2,1,2,32,128]{5,4,3,2,1,0:T(8,128)S(1)} %get-tuple-element.11), channel_id=1, source_target_pairs={{0,2},{2,0},{1,3},{3,1},{4,6},{6,4},{5,7},{7,5},{8,10},{10,8},{9,1... | collective-permute-start | bytes 3145736 | tf_op jit(solution)/shard_map/ppermute | solution.py:16
  493.5 26.1 %collective-permute-start.10 = (f32[16,2,1,2,32,128]{5,4,3,2,1,0:T(8,128)S(1)}, f32[16,2,1,2,32,128]{5,4,3,2,1,0:T(8,128)S(1)}, u32[]{:S(2)}, u32[]{:S(2)}) collective-permute-start(f32[16,2,1,2,32,128]{5,4,3,2,1,0:T(8,128)S(1)} %get-tuple-element.5), channel_id=1, source_target_pairs={{0,2},{2,0},{1,3},{3,1},{4,6},{6,4},{5,7},{7,5},{8,10},{10,8},{9,1... | collective-permute-start | bytes 3145736 | tf_op jit(solution)/shard_map/ppermute | solution.py:16
  494.9 46.8 %collective-permute-start.8 = (f32[16,1,1,4,32,128]{5,4,3,2,0,1:T(8,128)S(1)}, f32[16,1,1,4,32,128]{5,4,3,2,0,1:T(8,128)S(1)}, u32[]{:S(2)}, u32[]{:S(2)}) collective-permute-start(f32[16,1,1,4,32,128]{5,4,3,2,0,1:T(8,128)S(1)} %get-tuple-element.9), channel_id=1, source_target_pairs={{0,4},{4,0},{1,5},{5,1},{2,6},{6,2},{3,7},{7,3},{8,12},{12,8},{9,1... | collective-permute-start | bytes 3145736 | tf_op jit(solution)/shard_map/ppermute | solution.py:16
  520.0 41.5 %collective-permute-start.11 = (f32[16,1,1,4,32,128]{5,4,3,2,0,1:T(8,128)S(1)}, f32[16,1,1,4,32,128]{5,4,3,2,0,1:T(8,128)S(1)}, u32[]{:S(2)}, u32[]{:S(2)}) collective-permute-start(f32[16,1,1,4,32,128]{5,4,3,2,0,1:T(8,128)S(1)} %get-tuple-element.3), channel_id=1, source_target_pairs={{0,4},{4,0},{1,5},{5,1},{2,6},{6,2},{3,7},{7,3},{8,12},{12,8},{9,1... | collective-permute-start | bytes 3145736 | tf_op jit(solution)/shard_map/ppermute | solution.py:16
  561.5 2.3 copy-start.1
where the time goes:
time: 575 us; the launch traced here: 564 us
  waiting for transfers between devices  349 us (61%)
  matrix products  66.5 us (12%)
  starting transfers between devices  61.7 us (11%)
  other arithmetic  44.2 us (8%)
  local copies, waits for them, and re-layouts  41.4 us (7%)
    ppermute x12, waiting for transfers between devices, partner(): return lax.ppermute(block, axis, route)  186 us
    all_to_all x1, waiting for transfers between devices, body(): lax.all_to_all(pieces[0], 'wide', split_axis=2, concat_axis=0, tiled=True)  41.3 us
    all_to_all x1, waiting for transfers between devices, body(): lax.all_to_all(pieces[1], 'wide', split_axis=0, concat_axis=2, tiled=True)  41.2 us
    all_to_all x1, waiting for transfers between devices, body(): lax.all_to_all(pieces[1], 'wide', split_axis=2, concat_axis=0, tiled=True)  40.4 us
    all_to_all x1, waiting for transfers between devices, body(): lax.all_to_all(pieces[0], 'wide', split_axis=0, concat_axis=2, tiled=True)  39.5 us
    dot_general x1, matrix products, body(): jnp.dot(real_part, first_gate[1].T, precision=precise)  30.1 us
    add x1, other arithmetic, phase_turn(): real_part * sine + imag_part * cosine  26.3 us
    ppermute x12, starting transfers between devices, partner(): return lax.ppermute(block, axis, route)  20.9 us
  transfers between devices with their start and end apart: 16, of which 16 were waited for; matrix products, arithmetic and copies ran while one was open for 10% of the time, Pallas kernels for 0%

commit v1 on v0

v1 whole, which is shorter than its diff:
```python
import jax
import jax.numpy as jnp
from jax import lax
from jax.sharding import PartitionSpec as P

precise = lax.Precision.HIGHEST
close = lax.Precision.HIGH
AXES = ("wide", "narrow")


def ordered_gate(gate_pair, order_row):
    count = order_row.shape[0]
    states = jnp.arange(2**count, dtype=jnp.int32)
    places = jnp.arange(count, dtype=jnp.int32)
    digits = states[:, None] >> places[None, :] & 1
    mapped = jnp.sum(digits << order_row[None, :], axis=1)
    permute = (mapped[:, None] == states[None, :]).astype(jnp.float32)
    real_gate = jnp.dot(
        jnp.dot(permute, gate_pair[0], precision=precise), permute.T, precision=precise
    )
    imag_gate = jnp.dot(
        jnp.dot(permute, gate_pair[1], precision=precise), permute.T, precision=precise
    )
    return (real_gate, imag_gate)


def stacked(gate):
    return jnp.concatenate(
        [
            jnp.concatenate([gate[0], -gate[1]], axis=1),
            jnp.concatenate([gate[1], gate[0]], axis=1),
        ],
        axis=0,
    )


def phase_turn(real_part, imag_part, flat, phase_masks, phase_angles):
    angle_sum = jnp.zeros(real_part.shape, jnp.float32)
    for which in range(phase_masks.shape[0]):
        both = (flat & phase_masks[which, 0] != 0) & (flat & phase_masks[which, 1] != 0)
        angle_sum = angle_sum + jnp.where(both, phase_angles[which], 0.0)
    cosine = jnp.cos(angle_sum)
    sine = jnp.sin(angle_sum)
    return (real_part * cosine - imag_part * sine, real_part * sine + imag_part * cosine)


def body(state_real, state_imag, gates, gate_orders, phase_masks, phase_angles):
    real_part = state_real[0, 0]
    imag_part = state_imag[0, 0]
    rows, columns = real_part.shape
    first = ordered_gate(gates[0], gate_orders[0])
    second = stacked(ordered_gate(gates[1], gate_orders[1]))
    third = stacked(ordered_gate(gates[2], gate_orders[2]))
    both = jnp.concatenate([real_part, imag_part], axis=1)
    new = jnp.dot(both, stacked(first).T, precision=close)
    wide_count = lax.axis_size("wide")
    narrow_count = lax.axis_size("narrow")
    devices = wide_count * narrow_count
    high = rows // devices
    offset = (lax.axis_index("narrow") * wide_count + lax.axis_index("wide")) * (rows * columns)
    flat = (
        offset
        + jnp.arange(rows, dtype=jnp.int32)[:, None] * columns
        + jnp.arange(columns, dtype=jnp.int32)[None, :]
    )
    turned = phase_turn(new[:, :columns], new[:, columns:], flat, phase_masks, phase_angles)
    send = jnp.stack(turned).reshape(2, high, devices, columns).transpose(2, 0, 1, 3)
    got = lax.all_to_all(send, AXES, split_axis=0, concat_axis=0, tiled=True)
    inner = 128 // wide_count
    rest = high // inner
    view = got.reshape(wide_count, narrow_count, 2, inner, rest, columns)
    mid = jnp.dot(
        second, view.transpose(2, 0, 3, 1, 4, 5).reshape(256, -1), precision=close
    )
    mid = mid.reshape(2, wide_count, inner, narrow_count, rest, columns)
    out = jnp.dot(
        third, mid.transpose(0, 3, 2, 4, 1, 5).reshape(256, -1), precision=close
    )
    back = out.reshape(2, narrow_count, high, wide_count, columns).transpose(3, 1, 0, 2, 4)
    ret = lax.all_to_all(
        back.reshape(devices, 2, high, columns), AXES, split_axis=0, concat_axis=0, tiled=True
    )
    final = ret.transpose(1, 2, 0, 3).reshape(2, rows, columns)
    return (final[0][None, None], final[1][None, None])


def solution(mesh):
    placed = (P("narrow", "wide", None, None), P("narrow", "wide", None, None), P(), P(), P(), P())
    return jax.shard_map(
        body,
        mesh=mesh,
        in_specs=placed,
        out_specs=(P("narrow", "wide", None, None), P("narrow", "wide", None, None)),
        check_vma=False,
    )
```

time: 575 us -> 336 us (0.58); the launches traced: 564 us -> 333 us
  waiting for transfers between devices: 349 us -> 93.8 us
  blocking collectives: 0 us -> 104 us
  matrix products: 66.5 us -> 16.2 us
  starting transfers between devices: 61.7 us -> 15.7 us
  other arithmetic: 44.2 us -> 57.4 us
    ppermute x12 -> x0, waiting for transfers between devices: 186 us -> none  [partner(): return lax.ppermute(block, axis, route)]
    all_to_all x0 -> x1, blocking collectives: none -> 104 us  [body(): lax.all_to_all(back.reshape(devices, 2, high, columns), AXES, split_axis=...]
    all_to_all x4 -> x1, waiting for transfers between devices: 162 us -> 93.8 us  [body(): got = lax.all_to_all(send, AXES, split_axis=0, concat_axis=0, tiled=True)]
    dot_general x12 -> x3, matrix products: 61.8 us -> 11.7 us  [the longest x1 4.11 us: body(): new = jnp.dot(both, stacked(first).T, precision=close)]
    sub x0 -> x1, other arithmetic: none -> 27.4 us  [phase_turn(): real_part * cosine - imag_part * sine]
    all_to_all x4 -> x1, starting transfers between devices: 40.8 us -> 15.7 us  [body(): got = lax.all_to_all(send, AXES, split_axis=0, concat_axis=0, tiled=True)]
    ppermute x12 -> x0, starting transfers between devices: 20.9 us -> none  [partner(): return lax.ppermute(block, axis, route)]
    select_n x12 -> x0, other arithmetic: 17.6 us -> none  [swap_half(): jnp.where(own_bit == 0, jnp.concatenate([kept_half, arrived], axis=2), jn...]
  transfers between devices with their start and end apart: 16 -> 1, of which waited for: 16 -> 1; matrix products, arithmetic and copies ran while one was open for 10% -> 1% of each run, Pallas kernels for 0% -> 0%
where the time goes in v1:
time: 336 us; the launch traced here: 333 us
  blocking collectives  104 us (31%)
  waiting for transfers between devices  93.8 us (28%)
  other arithmetic  57.4 us (17%)
  local copies, waits for them, and re-layouts  44.6 us (13%)
  matrix products  16.2 us (5%)
  starting transfers between devices  15.7 us (5%)
    all_to_all x1, blocking collectives, body(): lax.all_to_all(back.reshape(devices, 2, high, columns), AXES, split_axis=...  104 us
    all_to_all x1, waiting for transfers between devices, body(): got = lax.all_to_all(send, AXES, split_axis=0, concat_axis=0, tiled=True)  93.8 us
    sub x1, other arithmetic, phase_turn(): real_part * cosine - imag_part * sine  27.4 us
    add x1, other arithmetic, phase_turn(): real_part * sine + imag_part * cosine  27.4 us
    all_to_all x1, starting transfers between devices, body(): got = lax.all_to_all(send, AXES, split_axis=0, concat_axis=0, tiled=True)  15.7 us
  transfers between devices with their start and end apart: 1, of which 1 were waited for; matrix products, arithmetic and copies ran while one was open for 1% of the time, Pallas kernels for 0%

profile of v1, /device:TPU:2, one launch (start us, length us, event | category | flops | bytes accessed | tf_op | source)
XLA Modules:
  0.0 332.8 jit_solution(14842011274777400646)
XLA Ops:
  0.6 0.8 slice_bitcast_fusion.1
  1.5 1.1 fusion.22
  2.6 1.1 fusion.24
  4.2 2.0 fusion.60
  6.2 1.6 fusion.61
  7.8 4.1 %fusion = f32[4096,256]{1,0:T(8,128)S(1)} fusion(f32[4096,128]{1,0:T(8,128)} %bitcast.111, f32[4096,128]{1,0:T(8,128)} %bitcast.112, f32[128,128]{0,1:T(8,128)S(1)} %fusion.37, f32[128,128]{0,1:T(8,128)S(1)} %get-tuple-element.34, f32[128,128]{0,1:T(8,128)S(1)} %get-tuple-element.33), kind=kOutput, calls=%fused_computation.1 | convolution fusion | flops 1611857920 | bytes 8585216 | tf_op jit(solution)/shard_map/dot_general | solution.py:55
  11.9 27.4 %multiply_subtract_fusion = f32[4096,128]{1,0:T(8,128)S(1)} fusion(f32[4096,256]{1,0:T(8,128)S(1)} %fusion, f32[]{:T(128)} %bitcast.38, s32[]{:T(128)} %bitcast.37, s32[]{:T(128)} %bitcast.36, f32[]{:T(128)} %bitcast.35, s32[]{:T(128)} %bitcast.34, s32[]{:T(128)} %bitcast.33, f32[]{:T(128)} %bitcast.32, s32[]{:T(128)} %bitcast.31, s32[]{:T(128)} %bitcast.30, ...), kind=kLoop, calls=%fused_computation.9 | loop fusion | flops 30932992 | bytes 6307936 | tf_op jit(solution)/shard_map/sub | solution.py:44
  39.4 27.4 %multiply_add_fusion = f32[4096,128]{1,0:T(8,128)S(1)} fusion(f32[4096,256]{1,0:T(8,128)S(1)} %fusion, f32[]{:T(128)} %bitcast.38, s32[]{:T(128)} %bitcast.37, s32[]{:T(128)} %bitcast.36, f32[]{:T(128)} %bitcast.35, s32[]{:T(128)} %bitcast.34, s32[]{:T(128)} %bitcast.33, f32[]{:T(128)} %bitcast.32, s32[]{:T(128)} %bitcast.31, s32[]{:T(128)} %bitcast.30, ...), kind=kLoop, calls=%fused_computation.8 | loop fusion | flops 30932992 | bytes 6307936 | tf_op jit(solution)/shard_map/add | solution.py:44
  66.8 1.2 copy.43
  68.0 1.2 copy.44
  69.3 2.3 maximum_bitcast_fusion
  71.6 15.7 %all-to-all-start = ((f32[256,2,16,128]{3,2,1,0:T(8,128)}), f32[256,2,16,128]{3,2,1,0:T(8,128)}, u32[]{:S(2)}, u32[]{:S(2)}) async-start(f32[256,2,16,128]{3,2,1,0:T(8,128)} %maximum_bitcast_fusion), calls=%async_computation | async-start | bytes 8388608 | tf_op jit(solution)/shard_map/all_to_all | solution.py:68
  89.8 93.8 %all-to-all-done = f32[256,2,16,128]{3,2,1,0:T(8,128)} async-done(((f32[256,2,16,128]{3,2,1,0:T(8,128)}), f32[256,2,16,128]{3,2,1,0:T(8,128)}, u32[]{:S(2)}, u32[]{:S(2)}) %all-to-all-start) | async-done | bytes 4194336 | tf_op jit(solution)/shard_map/all_to_all | solution.py:68
  183.6 4.6 %copy.45 = f32[256,2,16,128]{3,0,2,1:T(8,128)S(1)} copy(f32[256,2,16,128]{3,2,1,0:T(8,128)} %all-to-all-done) | data formatting | bytes 8388608 | tf_op jit(solution)/shard_map/all_to_all | solution.py:68
  188.2 4.7 %copy.46 = f32[2,32,4,8,4,128]{5,4,3,2,1,0:T(4,128)} copy(f32[2,32,4,8,4,128]{5,3,1,4,2,0:T(8,128)S(1)} %bitcast.102) | data formatting | bytes 8388608 | tf_op jit(solution)/shard_map/transpose | solution.py:73
  192.9 5.5 %reshape.55 = f32[256,4096]{1,0:T(8,128)} reshape(f32[2,32,4,8,4,128]{5,4,3,2,1,0:T(4,128)} %copy.46) | data formatting | bytes 8388608 | tf_op jit(solution)/shard_map/reshape | solution.py:73
  198.3 5.6 %copy.47 = f32[4096,256]{1,0:T(8,128)} copy(f32[4096,256]{0,1:T(8,128)} %bitcast.103) | data formatting | bytes 8388608 | tf_op jit(solution)/shard_map/dot_general | solution.py:72
  203.9 3.9 %convolution_bitcast_fusion.1 = f32[2,8,4,4,32,128]{5,4,3,1,2,0:T(8,128)S(1)} fusion(f32[8,4,128,256,1,1]{3,2,1,0,5,4:T(8,128)} %bitcast.100, f32[2,32,4,256,1,1]{3,2,1,0,5,4:T(4,128)S(1)} %bitcast.113), kind=kOutput, calls=%fused_computation.7 | convolution fusion | flops 1610612736 | bytes 8650752 | tf_op jit(solution)/shard_map/dot_general | solution.py:72
  208.7 5.7 %copy.65 = f32[32,8,32,128]{3,1,2,0:T(8,128)} copy(f32[32,8,32,128]{3,2,1,0:T(8,128)S(1)} %bitcast.104) | data formatting | bytes 8388608
  214.4 5.6 %copy.60 = f32[4096,256]{1,0:T(8,128)} copy(f32[4096,256]{0,1:T(8,128)} %bitcast.105) | data formatting | bytes 8388608 | tf_op jit(solution)/shard_map/dot_general | solution.py:76
  220.0 3.7 %convolution_bitcast_fusion = f32[32,8,2,16,128]{4,3,0,1,2:T(8,128)S(1)} fusion(f32[2,8,16,256,1]{3,2,4,1,0:T(8,128)S(1)} %bitcast.114, f32[32,128,256,1,1]{2,1,0,4,3:T(8,128)} %bitcast.101), kind=kOutput, calls=%fused_computation.6 | convolution fusion | flops 1610612736 | bytes 8650752 | tf_op jit(solution)/shard_map/dot_general | solution.py:76
  224.3 104.2 %all_to_all.10 = f32[256,2,16,128]{3,2,1,0:T(8,128)S(1)} all-to-all(f32[256,2,16,128]{3,2,1,0:T(8,128)S(1)} %bitcast.106), channel_id=1, replica_groups=mesh['wide'=32,'narrow'=8] {'wide','narrow'}, dimensions={0} | all-to-all | bytes 8388608 | tf_op jit(solution)/shard_map/all_to_all | solution.py:80
  328.9 2.0 copy.52
  330.9 2.0 copy.53
  (23 shorter events, 4.7 us)
Async XLA Ops:
  71.6 15.7 %copy-start = (f32[3,2,128,128]{3,2,1,0:T(8,128)S(1)}, f32[3,2,128,128]{3,2,1,0:T(8,128)}, u32[]{:S(2)}) copy-start(f32[3,2,128,128]{3,2,1,0:T(8,128)} %param.8) | copy-start | bytes 1179652
  71.6 112.0 %all-to-all-start = ((f32[256,2,16,128]{3,2,1,0:T(8,128)}), f32[256,2,16,128]{3,2,1,0:T(8,128)}, u32[]{:S(2)}, u32[]{:S(2)}) async-start(f32[256,2,16,128]{3,2,1,0:T(8,128)} %maximum_bitcast_fusion), calls=%async_computation | async-start | bytes 8388608 | tf_op jit(solution)/shard_map/all_to_all | solution.py:68

commit v2 on v1

v2 whole, which is shorter than its diff:
```python
import functools

import jax
import jax.numpy as jnp
from jax import lax
from jax.experimental import pallas as pl
from jax.experimental.pallas import tpu as pltpu
from jax.sharding import PartitionSpec as P

AXES = ("wide", "narrow")
QUBITS = 7
GATE = 128
f32 = jnp.float32
bf16 = jnp.bfloat16
VMEM = pl.BlockSpec(memory_space=pltpu.VMEM)
SMEM = pl.BlockSpec(memory_space=pltpu.SMEM)


def halves(value):
    high = value.astype(bf16)
    return high, (value - high.astype(f32)).astype(bf16)


def mul(left, right):
    return jnp.dot(left, right, preferred_element_type=f32)


def pick(states, orders_ref, row):
    mapped = jnp.zeros_like(states)
    for place in range(QUBITS):
        mapped = mapped + (((states >> place) & 1) << orders_ref[row, place])
    return (mapped == lax.broadcasted_iota(jnp.int32, (GATE, GATE), 1)).astype(bf16)


def chosen(left, right, gate):
    out = []
    for part in halves(gate):
        rows = mul(left, part).astype(bf16)
        out.append(
            lax.dot_general(rows, right, (((1,), (1,)), ((), ())), preferred_element_type=f32)
            .astype(bf16)
        )
    return out


def sincos(angle):
    turns = jnp.floor(angle * 0.6366197723675814 + 0.5)
    r = angle - turns * 1.5703125
    r = r - turns * 4.8351287841796875e-4
    r = r - turns * 3.13855707645416e-7
    s = r * r
    sine = r + r * s * (-1.6666654611e-1 + s * (8.3321608736e-3 - s * 1.9515295891e-4))
    cosine = 1.0 - 0.5 * s + s * s * (
        4.166664568298827e-2 + s * (-1.388731625493765e-3 + s * 2.443315711809948e-5)
    )
    quarter = turns.astype(jnp.int32)
    swap = (quarter & 1) == 1
    base_sin = jnp.where(swap, cosine, sine)
    base_cos = jnp.where(swap, sine, cosine)
    sine = jnp.where((quarter & 2) == 2, -base_sin, base_sin)
    cosine = jnp.where(((quarter + 1) & 2) == 2, -base_cos, base_cos)
    return sine, cosine


def front_kernel(base_ref, orders_ref, masks_ref, angles_ref, real_ref, imag_ref, gates_ref,
                 send_ref, high_ref, low_ref):
    devices = real_ref.shape[0] // 16
    states = lax.broadcasted_iota(jnp.int32, (GATE, GATE), 0)
    one_hot = pick(states, orders_ref, 0)
    real_high, real_low = chosen(one_hot, one_hot, gates_ref[0, 0])
    imag_high, imag_low = chosen(one_hot, one_hot, gates_ref[0, 1])
    for ref, real, imag in ((high_ref, real_high, imag_high), (low_ref, real_low, imag_low)):
        ref[:GATE, :GATE] = real
        ref[:GATE, GATE:] = -imag
        ref[GATE:, :GATE] = imag
        ref[GATE:, GATE:] = real

    def turned(left, right):
        return lax.dot_general(left, right, (((1,), (1,)), ((), ())), preferred_element_type=f32)

    shape = (devices, GATE)
    within = (
        lax.broadcasted_iota(jnp.int32, shape, 0) * GATE
        + lax.broadcasted_iota(jnp.int32, shape, 1)
    )

    @pl.loop(0, 16)
    def _(top):
        rows = pl.ds(pl.multiple_of(top * devices, devices), devices)
        both = jnp.concatenate([real_ref[rows, :], imag_ref[rows, :]], axis=1)
        x_high, x_low = halves(both)
        new = (
            turned(x_high, high_ref[...])
            + turned(x_high, low_ref[...])
            + turned(x_low, high_ref[...])
        )
        flat = within + (base_ref[0] + top * (devices * GATE))
        angle = jnp.zeros(shape, f32)
        for pair in range(masks_ref.shape[0]):
            mask = masks_ref[pair, 0] | masks_ref[pair, 1]
            angle = angle + jnp.where((flat & mask) == mask, angles_ref[pair], 0.0)
        sine, cosine = sincos(angle)
        real = new[:, :GATE]
        imag = new[:, GATE:]
        send_ref[pl.ds(top, devices, stride=32), :] = real * cosine - imag * sine
        send_ref[pl.ds(top + 16, devices, stride=32), :] = real * sine + imag * cosine


def middle_kernel(second_ref, third_ref, got_ref, back_ref, mid_ref):
    second_high, second_low = halves(second_ref[...])
    third_high, third_low = halves(third_ref[...])

    def apply(high, low, x):
        x_high, x_low = halves(x)
        return mul(high, x_high) + mul(low, x_high) + mul(high, x_low)

    @pl.loop(0, 16)
    def _(pair):
        sides = []
        for side in range(2):
            column = pair * 2 + side
            start = (column // 4) * 32 + column % 4
            sides.append(
                jnp.concatenate(
                    [
                        got_ref[pl.ds(start + part * 16 + inner * 4, 32, stride=256), :]
                        for part in range(2)
                        for inner in range(4)
                    ],
                    axis=0,
                )
            )
        out = apply(second_high, second_low, jnp.concatenate(sides, axis=1))
        for side in range(2):
            column = pair * 2 + side
            for part in range(2):
                rows = pl.ds(pl.multiple_of(part * 4096 + column * GATE, GATE), GATE)
                mid_ref[rows, :] = out[part * GATE : (part + 1) * GATE, side * GATE : (side + 1) * GATE]

    @pl.loop(0, 16)
    def _(pair):
        sides = []
        for side in range(2):
            sides.append(
                jnp.concatenate(
                    [
                        mid_ref[pl.ds(part * 4096 + pair * 2 + side, GATE, stride=32), :]
                        for part in range(2)
                    ],
                    axis=0,
                )
            )
        out = apply(third_high, third_low, jnp.concatenate(sides, axis=1))
        for side in range(2):
            rows = pl.ds(pl.multiple_of((pair * 2 + side) * 256, 256), 256)
            back_ref[rows, :] = out[:, side * GATE : (side + 1) * GATE]


def last_kernel(got_ref, real_ref, imag_ref):
    devices = real_ref.shape[0] // 16
    for part, ref in enumerate((real_ref, imag_ref)):

        @pl.loop(0, 16)
        def _(top):
            rows = pl.ds(pl.multiple_of(top * devices, devices), devices)
            ref[rows, :] = got_ref[pl.ds(top + part * 16, devices, stride=32), :]


def ordered(gate_pair, order_row, row_states, column_states):
    def one_hot(states):
        places = jnp.arange(QUBITS, dtype=jnp.int32)
        digits = states[:, None] >> places[None, :] & 1
        mapped = jnp.sum(digits << order_row[None, :], axis=1)
        return (mapped[:, None] == jnp.arange(GATE, dtype=jnp.int32)[None, :]).astype(f32)

    precise = lax.Precision.HIGHEST
    left, right = one_hot(row_states), one_hot(column_states)
    return [
        jnp.dot(jnp.dot(left, part, precision=precise), right.T, precision=precise)
        for part in (gate_pair[0], gate_pair[1])
    ]


def body(state_real, state_imag, gates, gate_orders, phase_masks, phase_angles):
    real_part = state_real[0, 0]
    imag_part = state_imag[0, 0]
    rows, columns = real_part.shape
    wide_count = lax.axis_size("wide")
    narrow_count = lax.axis_size("narrow")
    devices = wide_count * narrow_count
    base = (lax.axis_index("narrow") * wide_count + lax.axis_index("wide")) * (rows * columns)
    packed = jax.ShapeDtypeStruct((devices * 32, columns), f32)
    send = pl.pallas_call(
        front_kernel,
        out_shape=packed,
        in_specs=[SMEM] * 4 + [VMEM] * 3,
        out_specs=VMEM,
        scratch_shapes=[pltpu.VMEM((256, 256), bf16), pltpu.VMEM((256, 256), bf16)],
        name="front",
    )(base[None], gate_orders, phase_masks, phase_angles, real_part, imag_part, gates)

    def exchange(block):
        return lax.all_to_all(
            block.reshape(devices, 2, 16, columns), AXES, split_axis=0, concat_axis=0, tiled=True
        ).reshape(devices * 32, columns)

    got = exchange(send)
    states = jnp.arange(GATE, dtype=jnp.int32)
    by_inner = states % 32 * 4 + states // 32
    second = ordered(gates[1], gate_orders[1], by_inner, by_inner)
    swapped = states // 16 * 16 + states % 4 * 4 + states // 4 % 4
    third = ordered(gates[2], gate_orders[2], states, swapped)
    second = jnp.concatenate(
        [
            jnp.concatenate([second[0], -second[1]], axis=1),
            jnp.concatenate([second[1], second[0]], axis=1),
        ],
        axis=0,
    )
    third = jnp.stack(
        [
            jnp.concatenate([third[0], -third[1]], axis=1).reshape(8, 16, 256),
            jnp.concatenate([third[1], third[0]], axis=1).reshape(8, 16, 256),
        ],
        axis=1,
    ).reshape(256, 256)
    back = pl.pallas_call(
        middle_kernel,
        out_shape=packed,
        in_specs=[VMEM] * 3,
        out_specs=VMEM,
        scratch_shapes=[pltpu.VMEM((8192, GATE), f32)],
        name="middle",
    )(second, third, got)
    final = exchange(back)
    part = jax.ShapeDtypeStruct((rows, columns), f32)
    out_real, out_imag = pl.pallas_call(
        last_kernel,
        out_shape=(part, part),
        in_specs=[VMEM],
        out_specs=(VMEM, VMEM),
        name="last",
    )(final)
    return (out_real[None, None], out_imag[None, None])


def solution(mesh):
    placed = (P("narrow", "wide", None, None), P("narrow", "wide", None, None), P(), P(), P(), P())
    return jax.shard_map(
        body,
        mesh=mesh,
        in_specs=placed,
        out_specs=(P("narrow", "wide", None, None), P("narrow", "wide", None, None)),
        check_vma=False,
    )
```

time: 336 us -> 263 us (0.78)
  other arithmetic: 57.4 us -> 0.86 us
  local copies, waits for them, and re-layouts: 44.6 us -> 2.27 us
  Pallas kernels: 0 us -> 41.7 us
  matrix products: 16.2 us -> 1.97 us
    pallas_call x0 -> x3, Pallas kernels: none -> 41.7 us  [the longest x1 18 us: body(): pl.pallas_call(middle_kernel, out_shape=packed, in_specs=[VMEM] * 3, out_...]
    sub x1 -> x0, other arithmetic: 27.4 us -> none  [phase_turn(): real_part * cosine - imag_part * sine]
    add x2, other arithmetic: 27.4 us -> 0.01 us  [the longest x1 0.01 us: body(): swapped = states // 16 * 16 + states % 4 * 4 + states // 4 % 4]
    dot_general x15 -> x8, matrix products: 16.2 us -> 1.97 us  [the longest x4 1.05 us: ordered(): jnp.dot(jnp.dot(left, part, precision=precise), right.T, precision=precise)]
    dot_general x3 -> x0, local copies, waits for them, and re-layouts: 11.3 us -> none  [the longest x2 5.68 us: body(): jnp.dot(second, view.transpose(2, 0, 3, 1, 4, 5).reshape(256, -1), precis...]
    slice x5 -> x0, local copies, waits for them, and re-layouts: 7.86 us -> none  [the longest x3 4.25 us: body(): return (final[0][None, None], final[1][None, None])]
    transpose x3 -> x0, local copies, waits for them, and re-layouts: 6.11 us -> none  [the longest x1 4.67 us: body(): view.transpose(2, 0, 3, 1, 4, 5).reshape(256, -1)]
    reshape x1 -> x0, local copies, waits for them, and re-layouts: 5.47 us -> none  [body(): view.transpose(2, 0, 3, 1, 4, 5).reshape(256, -1)]
where the time goes in v2:
time: 263 us; the launch traced here: 261 us
  blocking collectives  105 us (40%)
  waiting for transfers between devices  92.4 us (35%)
  Pallas kernels  41.7 us (16%)
  starting transfers between devices  15.7 us (6%)
    all_to_all x1, blocking collectives, exchange(): lax.all_to_all(block.reshape(devices, 2, 16, columns), AXES, split_axis=0...  105 us
    all_to_all x1, waiting for transfers between devices, exchange(): lax.all_to_all(block.reshape(devices, 2, 16, columns), AXES, split_axis=0...  92.4 us
    pallas_call x1, Pallas kernels, body(): pl.pallas_call(middle_kernel, out_shape=packed, in_specs=[VMEM] * 3, out_...  18 us
    all_to_all x1, starting transfers between devices, exchange(): lax.all_to_all(block.reshape(devices, 2, 16, columns), AXES, split_axis=0...  15.7 us
    pallas_call x1, Pallas kernels, body(): pl.pallas_call(front_kernel, out_shape=packed, in_specs=[SMEM] * 4 + [VME...  15.1 us
    pallas_call x1, Pallas kernels, body(): pl.pallas_call(last_kernel, out_shape=(part, part), in_specs=[VMEM], out_...  8.62 us
  transfers between devices with their start and end apart: 1, of which 1 were waited for; matrix products, arithmetic and copies ran while one was open for 1% of the time, Pallas kernels for 0%

profile of v2, /device:TPU:2, one launch (start us, length us, event | category | flops | bytes accessed | tf_op | source)
XLA Modules:
  0.0 261.0 jit_solution(6682326977285064566)
XLA Ops:
  0.6 1.3 copy.30.masks_ref
  2.0 15.1 %front.1 = f32[8192,128]{1,0:T(8,128)} custom-call(s32[1]{0:T(128)} %bitcast.9.base_ref, s32[3,7]{1,0:T(4,128)} %orders_ref.1, s32[8,2]{1,0:T(8,128)} %copy.30.masks_ref, f32[8]{0:T(128)} %angles_ref.1, f32[4096,128]{1,0:T(8,128)} %bitcast.35, f32[4096,128]{1,0:T(8,128)} %bitcast.36, f32[3,2,128,128]{3,2,1,0:T(8,128)} %gates_ref.1), custom_call_target="tpu_custom_call" | custom-call | tf_op jit(solution)/shard_map/front/pallas_call | solution.py:193
  17.1 0.0 copy-start.1
  17.1 0.0 copy-start
  17.1 15.7 %all-to-all-start = ((f32[256,2,16,128]{3,2,1,0:T(8,128)}), f32[256,2,16,128]{3,2,1,0:T(8,128)}, u32[]{:S(2)}, u32[]{:S(2)}) async-start(f32[256,2,16,128]{3,2,1,0:T(8,128)} %bitcast.32), calls=%async_computation | async-start | bytes 8388608 | tf_op jit(solution)/shard_map/all_to_all | solution.py:203
  32.8 0.0 copy-done.1
  32.8 0.1 shift-left_reduce_fusion
  32.9 0.0 copy-done
  32.9 0.2 fusion
  33.1 0.2 fusion.2
  33.4 0.2 fusion.10
  33.6 0.2 fusion.33
  33.9 0.1 copy.27
  34.0 0.1 copy.28
  34.1 0.7 copy.29
  34.9 0.2 fusion.4
  35.1 0.2 fusion.6
  35.3 0.3 fusion.15
  35.6 0.3 fusion.32
  35.9 0.7 maximum_maximum_fusion.second_ref
  36.6 92.4 %all-to-all-done = f32[256,2,16,128]{3,2,1,0:T(8,128)} async-done(((f32[256,2,16,128]{3,2,1,0:T(8,128)}), f32[256,2,16,128]{3,2,1,0:T(8,128)}, u32[]{:S(2)}, u32[]{:S(2)}) %all-to-all-start) | async-done | bytes 4194336 | tf_op jit(solution)/shard_map/all_to_all | solution.py:203
  129.1 18.0 %middle.1 = f32[8192,128]{1,0:T(8,128)} custom-call(f32[256,256]{1,0:T(8,128)} %maximum_maximum_fusion.second_ref, f32[256,256]{1,0:T(8,128)} %bitcast.37, f32[8192,128]{1,0:T(8,128)} %bitcast.13.got_ref), custom_call_target="tpu_custom_call" | custom-call | tf_op jit(solution)/shard_map/middle/pallas_call | solution.py:227
  147.0 105.3 %all_to_all.10 = f32[256,2,16,128]{3,2,1,0:T(8,128)} all-to-all(f32[256,2,16,128]{3,2,1,0:T(8,128)} %bitcast.33), channel_id=1, replica_groups=mesh['wide'=32,'narrow'=8] {'wide','narrow'}, dimensions={0} | all-to-all | bytes 8388608 | tf_op jit(solution)/shard_map/all_to_all | solution.py:203
  252.4 8.6 %last.1 = (f32[4096,128]{1,0:T(8,128)}, f32[4096,128]{1,0:T(8,128)}) custom-call(f32[8192,128]{1,0:T(8,128)} %bitcast.34), custom_call_target="tpu_custom_call" | custom-call | tf_op jit(solution)/shard_map/last/pallas_call | solution.py:237
  (5 shorter events, 0.1 us)
Async XLA Ops:
  17.1 15.7 %copy-start.1 = (s32[3,7]{1,0:T(4,128)S(1)}, s32[3,7]{1,0:T(4,128)}, u32[]{:S(2)}) copy-start(s32[3,7]{1,0:T(4,128)} %orders_ref.1) | copy-start | bytes 256
  17.1 15.8 %copy-start = (f32[3,2,128,128]{3,2,1,0:T(8,128)S(1)}, f32[3,2,128,128]{3,2,1,0:T(8,128)}, u32[]{:S(2)}) copy-start(f32[3,2,128,128]{3,2,1,0:T(8,128)} %gates_ref.1) | copy-start | bytes 1179652
  17.1 112.0 %all-to-all-start = ((f32[256,2,16,128]{3,2,1,0:T(8,128)}), f32[256,2,16,128]{3,2,1,0:T(8,128)}, u32[]{:S(2)}, u32[]{:S(2)}) async-start(f32[256,2,16,128]{3,2,1,0:T(8,128)} %bitcast.32), calls=%async_computation | async-start | bytes 8388608 | tf_op jit(solution)/shard_map/all_to_all | solution.py:203

commit v3 on v2

v3 whole, which is shorter than its diff:
```python
import jax
import jax.numpy as jnp
from jax import lax
from jax.experimental import pallas as pl
from jax.experimental.pallas import tpu as pltpu
from jax.sharding import Mesh
from jax.sharding import PartitionSpec as P


PLANE = ("x", "c", "y")
DEPTH = ("zh", "zl")
QUBITS = 7
GATE = 128
f32 = jnp.float32
bf16 = jnp.bfloat16
VMEM = pl.BlockSpec(memory_space=pltpu.VMEM)
SMEM = pl.BlockSpec(memory_space=pltpu.SMEM)


def halves(value):
    high = value.astype(bf16)
    return high, (value - high.astype(f32)).astype(bf16)


def mul(left, right):
    return jnp.dot(left, right, preferred_element_type=f32)


def pick(states, orders_ref, row):
    mapped = jnp.zeros_like(states)
    for place in range(QUBITS):
        mapped = mapped + (((states >> place) & 1) << orders_ref[row, place])
    return (mapped == lax.broadcasted_iota(jnp.int32, (GATE, GATE), 1)).astype(bf16)


def chosen(left, right, gate):
    out = []
    for part in halves(gate):
        rows = mul(left, part).astype(bf16)
        out.append(
            lax.dot_general(rows, right, (((1,), (1,)), ((), ())), preferred_element_type=f32)
            .astype(bf16)
        )
    return out


def sincos(angle):
    turns = jnp.floor(angle * 0.6366197723675814 + 0.5)
    r = angle - turns * 1.5703125
    r = r - turns * 4.8351287841796875e-4
    r = r - turns * 3.13855707645416e-7
    s = r * r
    sine = r + r * s * (-1.6666654611e-1 + s * (8.3321608736e-3 - s * 1.9515295891e-4))
    cosine = 1.0 - 0.5 * s + s * s * (
        4.166664568298827e-2 + s * (-1.388731625493765e-3 + s * 2.443315711809948e-5)
    )
    quarter = turns.astype(jnp.int32)
    swap = (quarter & 1) == 1
    base_sin = jnp.where(swap, cosine, sine)
    base_cos = jnp.where(swap, sine, cosine)
    sine = jnp.where((quarter & 2) == 2, -base_sin, base_sin)
    cosine = jnp.where(((quarter + 1) & 2) == 2, -base_cos, base_cos)
    return sine, cosine


def front_kernel(
    base_ref, me_ref, orders_ref, masks_ref, angles_ref, real_ref, imag_ref, gates_ref, *rest
):
    slab_refs, flat_ref, high_ref, low_ref, depth_ref = rest[:8], rest[8], rest[9], rest[10], rest[11]
    states = lax.broadcasted_iota(jnp.int32, (GATE, GATE), 0)
    one_hot = pick(states, orders_ref, 0)
    real_high, real_low = chosen(one_hot, one_hot, gates_ref[0, 0])
    imag_high, imag_low = chosen(one_hot, one_hot, gates_ref[0, 1])
    for ref, real, imag in ((high_ref, real_high, imag_high), (low_ref, real_low, imag_low)):
        ref[:GATE, :GATE] = real
        ref[:GATE, GATE:] = -imag
        ref[GATE:, :GATE] = imag
        ref[GATE:, GATE:] = real

    def turned(left, right):
        return lax.dot_general(left, right, (((1,), (1,)), ((), ())), preferred_element_type=f32)

    shape = (256, GATE)
    lane = lax.broadcasted_iota(jnp.int32, shape, 1)
    within = lax.broadcasted_iota(jnp.int32, shape, 0) * GATE + lane
    lower = lane < 64

    @pl.loop(0, 16)
    def _(top):
        rows = pl.ds(pl.multiple_of(top * 256, 256), 256)
        both = jnp.concatenate([real_ref[rows, :], imag_ref[rows, :]], axis=1)
        x_high, x_low = halves(both)
        new = (
            turned(x_high, high_ref[...])
            + turned(x_high, low_ref[...])
            + turned(x_low, high_ref[...])
        )
        flat = within + (base_ref[0] + top * (256 * GATE))
        angle = jnp.zeros(shape, f32)
        for pair in range(masks_ref.shape[0]):
            mask = masks_ref[pair, 0] | masks_ref[pair, 1]
            angle = angle + jnp.where((flat & mask) == mask, angles_ref[pair], 0.0)
        sine, cosine = sincos(angle)
        real = new[:, :GATE]
        imag = new[:, GATE:]
        real, imag = real * cosine - imag * sine, real * sine + imag * cosine
        depth_ref[pl.ds(top, 256, stride=16), :] = jnp.where(lower, real, pltpu.roll(imag, 64, 1))
        flat_ref[pl.ds(top, 256, stride=16), :] = jnp.where(lower, pltpu.roll(real, 64, 1), imag)

    spread(depth_ref, me_ref, slab_refs)


def spread(depth_ref, me_ref, slab_refs):
    for shift, ref in enumerate(slab_refs):
        start = ((me_ref[0] + shift) & 7) * 512
        ref[...] = depth_ref[pl.ds(pl.multiple_of(start, 512), 512), :]


def gather_in(slab_refs, me_ref, depth_ref):
    for shift, ref in enumerate(slab_refs):
        start = ((me_ref[0] - shift) & 7) * 512
        depth_ref[pl.ds(pl.multiple_of(start, 512), 512), :] = ref[...]


def apply_gates(second_ref, third_ref, got_ref, back_ref, mid_ref, depth, plane):
    second_high, second_low = halves(second_ref[...])
    third_high, third_low = halves(third_ref[...])
    lower = lax.broadcasted_iota(jnp.int32, (GATE, GATE), 1) < 64

    def with_turned(x):
        other = pltpu.roll(x, 64, 1)
        return jnp.concatenate([x, jnp.where(lower, -other, other)], axis=0)

    def apply(high, low, x):
        x_high, x_low = halves(x)
        return mul(high, x_high) + mul(low, x_high) + mul(high, x_low)

    @pl.loop(0, 16)
    def _(pair):
        sides = []
        for side in range(2):
            column = pair * 2 + side
            start = (column // 8) * plane + (column // 4 % 2) * depth + column % 4
            sides.append(
                with_turned(
                    jnp.concatenate(
                        [
                            got_ref[pl.ds(start + zh * 2 * depth + inner * 4, 8, stride=4 * plane), :]
                            for inner in range(4)
                            for zh in range(4)
                        ],
                        axis=0,
                    )
                )
            )
        out = apply(second_high, second_low, jnp.concatenate(sides, axis=1))
        for side in range(2):
            rows = pl.ds(pl.multiple_of((pair * 2 + side) * GATE, GATE), GATE)
            mid_ref[rows, :] = out[:, side * GATE : (side + 1) * GATE]

    @pl.loop(0, 16)
    def _(pair):
        sides = [
            with_turned(mid_ref[pl.ds(pair * 2 + side, GATE, stride=32), :]) for side in range(2)
        ]
        out = apply(third_high, third_low, jnp.concatenate(sides, axis=1))
        for side in range(2):
            wide = pair * 2 + side
            start = (wide // 8) * 2 * depth + (wide % 8) * 4 * plane
            for narrow in range(8):
                rows = pl.ds(
                    pl.multiple_of(start + narrow // 2 * plane + narrow % 2 * depth, 16), 16
                )
                back_ref[rows, :] = out[
                    narrow * 16 : (narrow + 1) * 16, side * GATE : (side + 1) * GATE
                ]


def flat_kernel(second_ref, third_ref, got_ref, back_ref, mid_ref):
    apply_gates(second_ref, third_ref, got_ref, back_ref, mid_ref, 16, 128)


def depth_kernel(me_ref, second_ref, third_ref, *rest):
    slab_refs, back_refs, depth_ref, mid_ref = rest[:8], rest[8:16], rest[16], rest[17]
    gather_in(slab_refs, me_ref, depth_ref)
    apply_gates(second_ref, third_ref, depth_ref, depth_ref, mid_ref, 512, 16)
    spread(depth_ref, me_ref, back_refs)


def split_kernel(me_ref, flat_ref, *slab_refs):
    for shift, ref in enumerate(slab_refs):
        ref[...] = flat_ref[:, (me_ref[0] + shift) & 7]


def join_kernel(me_ref, *refs):
    for shift, ref in enumerate(refs[:8]):
        refs[8][:, (me_ref[0] - shift) & 7] = ref[...]


def last_kernel(me_ref, *rest):
    slab_refs, flat_ref, real_ref, imag_ref, depth_ref = rest[:8], rest[8], rest[9], rest[10], rest[11]
    gather_in(slab_refs, me_ref, depth_ref)
    lower = lax.broadcasted_iota(jnp.int32, (256, GATE), 1) < 64

    @pl.loop(0, 16)
    def _(top):
        rows = pl.ds(pl.multiple_of(top * 256, 256), 256)
        first = depth_ref[pl.ds(top, 256, stride=16), :]
        second = flat_ref[pl.ds(top, 256, stride=16), :]
        real_ref[rows, :] = jnp.where(lower, first, pltpu.roll(second, 64, 1))
        imag_ref[rows, :] = jnp.where(lower, pltpu.roll(first, 64, 1), second)


def ordered(gate_pair, order_row, row_states, column_states):
    def one_hot(states):
        places = jnp.arange(QUBITS, dtype=jnp.int32)
        digits = states[:, None] >> places[None, :] & 1
        mapped = jnp.sum(digits << order_row[None, :], axis=1)
        return (mapped[:, None] == jnp.arange(GATE, dtype=jnp.int32)[None, :]).astype(f32)

    precise = lax.Precision.HIGHEST
    left, right = one_hot(row_states), one_hot(column_states)
    return [
        jnp.dot(jnp.dot(left, part, precision=precise), right.T, precision=precise)
        for part in (gate_pair[0], gate_pair[1])
    ]


def body(state_real, state_imag, gates, gate_orders, phase_masks, phase_angles):
    real_part = state_real[0, 0]
    imag_part = state_imag[0, 0]
    rows, columns = real_part.shape
    wide = ("x", "zh", "c")
    narrow = ("y", "zl")
    base = (lax.axis_index(narrow) * lax.axis_size(wide) + lax.axis_index(wide)) * (rows * columns)
    me = lax.axis_index(DEPTH)[None]
    whole = jax.ShapeDtypeStruct((rows, columns), f32)
    grouped = jax.ShapeDtypeStruct((32, 8, 16, columns), f32)
    slab = jax.ShapeDtypeStruct((512, columns), f32)
    block = jax.ShapeDtypeStruct((32, 16, columns), f32)
    room = pltpu.VMEM((rows, columns), f32)

    def call(kernel, out_shape, scalars, arrays, scratch=(), work=1, after=()):
        outs = (VMEM,) * len(out_shape) if isinstance(out_shape, tuple) else VMEM
        first = len(scalars) + len(arrays)

        def run(*refs):
            kernel(*refs[:first], *refs[first + len(after) :])

        return pl.pallas_call(
            run,
            out_shape=out_shape,
            in_specs=[SMEM] * len(scalars)
            + [VMEM] * len(arrays)
            + [pl.BlockSpec(memory_space=pl.ANY)] * len(after),
            out_specs=outs,
            scratch_shapes=list(scratch),
            cost_estimate=pl.CostEstimate(
                flops=work * 10**9, bytes_accessed=work * 4 * 2**20, transcendentals=0
            ),
        )(*scalars, *arrays, *after)

    def along(slabs):
        moved = [slabs[0]]
        for shift in range(1, 8):
            route = [(z, (z + shift) % 8) for z in range(8)]
            moved.append(lax.ppermute(slabs[shift], DEPTH, route))
        return moved

    def across(array):
        return lax.all_to_all(
            array.reshape(32, 128, columns), PLANE, split_axis=0, concat_axis=0, tiled=True
        )

    *slabs, flat = call(
        front_kernel,
        (slab,) * 8 + (whole,),
        [base[None], me, gate_orders, phase_masks, phase_angles],
        [real_part, imag_part, gates],
        [pltpu.VMEM((256, 256), bf16), pltpu.VMEM((256, 256), bf16), room],
        work=3,
    )
    states = jnp.arange(GATE, dtype=jnp.int32)
    zh, xc = states // 8 % 4, states % 8
    inner = states // 32
    column_states = ((xc // 2 * 8) + zh * 2 + xc % 2) * 4 + inner
    spot = states % 32
    row_states = (spot % 8 // 2 * 8 + spot // 8 * 2 + spot % 2) * 4 + inner
    second = jnp.concatenate(ordered(gates[1], gate_orders[1], row_states, column_states), axis=1)
    swapped = states // 16 * 16 + states % 4 * 4 + states // 4 % 4
    third = jnp.concatenate(ordered(gates[2], gate_orders[2], states, swapped), axis=1)

    slabs = along(slabs)
    flat = across(flat)
    pieces = call(split_kernel, (block,) * 8, [me], [flat.reshape(32, 8, 16, columns)])
    last_sent = pieces[7]
    pieces = along([piece.reshape(512, columns) for piece in pieces])
    slabs = [piece.reshape(32, 16, columns) for piece in slabs]
    joined = call(join_kernel, grouped, [me], slabs, after=[last_sent])
    joined = across(joined).reshape(rows, columns)
    joined = call(flat_kernel, whole, [], [second, third, joined], [room], work=2)
    pieces = call(
        depth_kernel,
        (slab,) * 8,
        [me],
        [second, third, *pieces],
        [room, room],
        work=2,
        after=[joined],
    )
    pieces = along(pieces)
    joined = across(joined)
    slabs = call(split_kernel, (block,) * 8, [me], [joined.reshape(32, 8, 16, columns)])
    last_sent = slabs[7]
    slabs = along([piece.reshape(512, columns) for piece in slabs])
    pieces = [piece.reshape(32, 16, columns) for piece in pieces]
    flat = call(join_kernel, grouped, [me], pieces, after=[last_sent])
    flat = across(flat).reshape(rows, columns)
    out_real, out_imag = call(last_kernel, (whole, whole), [me], [*slabs, flat], [room], work=2)
    return (out_real[None, None], out_imag[None, None])


def solution(mesh):
    fine = Mesh(mesh.devices.reshape(4, 4, 2, 4, 2), ("x", "zh", "c", "y", "zl"))
    state = P(("y", "zl"), ("x", "zh", "c"), None, None)
    return jax.shard_map(
        body,
        mesh=fine,
        in_specs=(state, state, P(), P(), P(), P()),
        out_specs=(state, state),
        check_vma=False,
    )
```

time: 263 us -> 344 us (1.31)
  blocking collectives: 105 us -> 0 us
  waiting for transfers between devices: 92.4 us -> 172 us
  starting transfers between devices: 15.7 us -> 94.4 us
  Pallas kernels: 41.7 us -> 63.8 us
  local copies, waits for them, and re-layouts: 2.27 us -> 8.19 us
    ppermute x0 -> x28, waiting for transfers between devices: none -> 148 us  [along(): moved.append(lax.ppermute(slabs[shift], DEPTH, route))]
    all_to_all x1 -> x0, blocking collectives: 105 us -> none  [exchange(): lax.all_to_all(block.reshape(devices, 2, 16, columns), AXES, split_axis=0...]
    all_to_all x1 -> x4, waiting for transfers between devices: 92.4 us -> 23.8 us  [across(): lax.all_to_all(array.reshape(32, 128, columns), PLANE, split_axis=0, conc...]
    ppermute x0 -> x28, starting transfers between devices: none -> 65.3 us  [along(): moved.append(lax.ppermute(slabs[shift], DEPTH, route))]
    pallas_call x3 -> x8, Pallas kernels: 41.7 us -> 63.8 us  [call(): pl.pallas_call(run, out_shape=out_shape, in_specs=[SMEM] * len(scalars) +...]
    all_to_all x1 -> x4, starting transfers between devices: 15.7 us -> 29.1 us  [across(): lax.all_to_all(array.reshape(32, 128, columns), PLANE, split_axis=0, conc...]
    unnamed x5 -> x79, local copies, waits for them, and re-layouts: 1.35 us -> 8.19 us
  transfers between devices with their start and end apart: 1 -> 32, of which waited for: 1 -> 22; matrix products, arithmetic and copies ran while one was open for 1% -> 1% of each run, Pallas kernels for 0% -> 6%
where the time goes in v3:
time: 344 us; the launch traced here: 343 us
  waiting for transfers between devices  172 us (50%)
  starting transfers between devices  94.4 us (27%)
  Pallas kernels  63.8 us (19%)
  local copies, waits for them, and re-layouts  8.19 us (2%)
    ppermute x28, waiting for transfers between devices, along(): moved.append(lax.ppermute(slabs[shift], DEPTH, route))  148 us
    ppermute x28, starting transfers between devices, along(): moved.append(lax.ppermute(slabs[shift], DEPTH, route))  65.3 us
    pallas_call x8, Pallas kernels, call(): pl.pallas_call(run, out_shape=out_shape, in_specs=[SMEM] * len(scalars) +...  63.8 us
    all_to_all x4, starting transfers between devices, across(): lax.all_to_all(array.reshape(32, 128, columns), PLANE, split_axis=0, conc...  29.1 us
    all_to_all x4, waiting for transfers between devices, across(): lax.all_to_all(array.reshape(32, 128, columns), PLANE, split_axis=0, conc...  23.8 us
    unnamed x79, local copies, waits for them, and re-layouts  8.19 us
  transfers between devices with their start and end apart: 32, of which 22 were waited for; matrix products, arithmetic and copies ran while one was open for 1% of the time, Pallas kernels for 6%

profile of v3, /device:TPU:2, one launch (start us, length us, event | category | flops | bytes accessed | tf_op | source)
XLA Modules:
  0.0 342.5 jit_solution(2985653106262364393)
XLA Ops:
  2.0 15.9 %shard_map.77 = (f32[512,128]{1,0:T(8,128)}, f32[512,128]{1,0:T(8,128)}, f32[512,128]{1,0:T(8,128)}, f32[512,128]{1,0:T(8,128)}, f32[512,128]{1,0:T(8,128)}, /*i...) custom-call(s32[1]{0:T(128)} %bitcast.7.refs_0_, s32[1]{0:T(128)} %bitcast.refs_1_.refs_0_, ...), custom_call_target="tpu_custom_call" | custom-call | flops 3000000000 | bytes 12582912 | tf_op jit(solution)/shard_map/pallas_call | solution.py:250
  17.9 7.8 %all-to-all-start = ((f32[32,128,128]{2,1,0:T(8,128)}), f32[32,128,128]{2,1,0:T(8,128)S(1)}, u32[]{:S(2)}, u32[]{:S(2)}) async-start(f32[32,128,128]{2,1,0:T(8,128)} %bitcast.72), calls=%async_computation | async-start | bytes 4194304 | tf_op jit(solution)/shard_map/all_to_all | solution.py:271
  40.5 6.3 %collective-permute-start.5 = (f32[512,128]{1,0:T(8,128)}, f32[512,128]{1,0:T(8,128)}, u32[]{:S(2)}, u32[]{:S(2)}) collective-permute-start(f32[512,128]{1,0:T(8,128)} %get-tuple-element.43), channel_id=1, source_target_pairs={{0,48},{1,49},{16,0},{17,1},{32,16},{33,17},{48,32},{49,33},{2,50}... | collective-permute-start | bytes 786440 | tf_op jit(solution)/shard_map/ppermute | solution.py:267
  46.8 6.0 %collective-permute-done.1 = f32[512,128]{1,0:T(8,128)S(1)} collective-permute-done((f32[512,128]{1,0:T(8,128)}, f32[512,128]{1,0:T(8,128)S(1)}, u32[]{:S(2)}, u32[]{:S(2)}) %collective-permute-start.1) | collective-permute-done | bytes 262176 | tf_op jit(solution)/shard_map/ppermute | solution.py:267
  60.2 12.1 %collective-permute-done.2 = f32[512,128]{1,0:T(8,128)S(1)} collective-permute-done((f32[512,128]{1,0:T(8,128)}, f32[512,128]{1,0:T(8,128)S(1)}, u32[]{:S(2)}, u32[]{:S(2)}) %collective-permute-start.2) | collective-permute-done | bytes 262176 | tf_op jit(solution)/shard_map/ppermute | solution.py:267
  72.3 7.1 %collective-permute-done.5 = f32[512,128]{1,0:T(8,128)} collective-permute-done((f32[512,128]{1,0:T(8,128)}, f32[512,128]{1,0:T(8,128)}, u32[]{:S(2)}, u32[]{:S(2)}) %collective-permute-start.5) | collective-permute-done | bytes 262176 | tf_op jit(solution)/shard_map/ppermute | solution.py:267
  85.6 7.5 %all-to-all-start.1 = ((f32[32,128,128]{2,1,0:T(8,128)}), f32[32,128,128]{2,1,0:T(8,128)S(1)}, u32[]{:S(2)}, u32[]{:S(2)}) async-start(f32[32,128,128]{2,1,0:T(8,128)} %bitcast.67), calls=%async_computation.1 | async-start | bytes 4194304 | tf_op jit(solution)/shard_map/all_to_all | solution.py:271
  96.6 23.8 %all-to-all-done.1 = f32[32,128,128]{2,1,0:T(8,128)S(1)} async-done(((f32[32,128,128]{2,1,0:T(8,128)}), f32[32,128,128]{2,1,0:T(8,128)S(1)}, u32[]{:S(2)}, u32[]{:S(2)}) %all-to-all-start.1) | async-done | bytes 2097184 | tf_op jit(solution)/shard_map/all_to_all | solution.py:271
  121.7 14.0 %shard_map.80.refs_11_ = f32[4096,128]{1,0:T(8,128)} custom-call(f32[128,256]{1,0:T(8,128)} %pad_maximum_fusion.refs_0_.refs_1_, f32[128,256]{1,0:T(8,128)} %pad_maximum_fusion.1.refs_1_.refs_2_, f32[4096,128]{1,0:T(8,128)} %bitcast.73), custom_call_target="tpu_custom_call" | custom-call | flops 2000000000 | bytes 8388608 | tf_op jit(solution)/shard_map/pallas_call | solution.py:250
  135.7 6.3 %all-to-all-start.2 = ((f32[32,128,128]{2,1,0:T(8,128)}), f32[32,128,128]{2,1,0:T(8,128)S(1)}, u32[]{:S(2)}, u32[]{:S(2)}) async-start(f32[32,128,128]{2,1,0:T(8,128)} %bitcast.69), calls=%async_computation.2 | async-start | bytes 4194304 | tf_op jit(solution)/shard_map/all_to_all | solution.py:271
  156.0 14.4 %collective-permute-done.15.refs_5_ = f32[512,128]{1,0:T(8,128)S(1)} collective-permute-done((f32[512,128]{1,0:T(8,128)}, f32[512,128]{1,0:T(8,128)S(1)}, u32[]{:S(2)}, u32[]{:S(2)}) %collective-permute-start.15) | collective-permute-done | bytes 262176 | tf_op jit(solution)/shard_map/ppermute | solution.py:267
  170.5 10.2 %collective-permute-done.16.refs_6_ = f32[512,128]{1,0:T(8,128)S(1)} collective-permute-done((f32[512,128]{1,0:T(8,128)S(1)}, f32[512,128]{1,0:T(8,128)S(1)}, u32[]{:S(2)}, u32[]{:S(2)}) %collective-permute-start.16) | collective-permute-done | bytes 262176 | tf_op jit(solution)/shard_map/ppermute | solution.py:267
  180.6 9.8 %collective-permute-done.17.refs_7_ = f32[512,128]{1,0:T(8,128)S(1)} collective-permute-done((f32[512,128]{1,0:T(8,128)S(1)}, f32[512,128]{1,0:T(8,128)S(1)}, u32[]{:S(2)}, u32[]{:S(2)}) %collective-permute-start.17) | collective-permute-done | bytes 262176 | tf_op jit(solution)/shard_map/ppermute | solution.py:267
  192.5 5.6 %collective-permute-done.20.refs_10_ = f32[512,128]{1,0:T(8,128)S(1)} collective-permute-done((f32[512,128]{1,0:T(8,128)S(1)}, f32[512,128]{1,0:T(8,128)S(1)}, u32[]{:S(2)}, u32[]{:S(2)}) %collective-permute-start.20) | collective-permute-done | bytes 262176 | tf_op jit(solution)/shard_map/ppermute | solution.py:267
  198.8 14.1 %shard_map.82 = (f32[512,128]{1,0:T(8,128)}, f32[512,128]{1,0:T(8,128)}, f32[512,128]{1,0:T(8,128)}, f32[512,128]{1,0:T(8,128)}, f32[512,128]{1,0:T(8,128)}, /*i...) custom-call(s32[1]{0:T(128)} %bitcast.refs_1_.refs_0_, f32[128,256]{1,0:T(8,128)} %pad_maximum_fusion.refs_0_.refs_1_, ...), custom_call_target="tpu_custom_call" | custom-call | flops 2000000000 | bytes 8388608 | tf_op jit(solution)/shard_map/pallas_call | solution.py:250
  228.2 9.4 %collective-permute-done.22 = f32[512,128]{1,0:T(8,128)S(1)} collective-permute-done((f32[512,128]{1,0:T(8,128)}, f32[512,128]{1,0:T(8,128)S(1)}, u32[]{:S(2)}, u32[]{:S(2)}) %collective-permute-start.22) | collective-permute-done | bytes 262176 | tf_op jit(solution)/shard_map/ppermute | solution.py:267
  242.1 8.1 %collective-permute-done.23 = f32[512,128]{1,0:T(8,128)S(1)} collective-permute-done((f32[512,128]{1,0:T(8,128)}, f32[512,128]{1,0:T(8,128)S(1)}, u32[]{:S(2)}, u32[]{:S(2)}) %collective-permute-start.23) | collective-permute-done | bytes 262176 | tf_op jit(solution)/shard_map/ppermute | solution.py:267
  250.2 11.8 %collective-permute-done.24 = f32[512,128]{1,0:T(8,128)S(1)} collective-permute-done((f32[512,128]{1,0:T(8,128)}, f32[512,128]{1,0:T(8,128)S(1)}, u32[]{:S(2)}, u32[]{:S(2)}) %collective-permute-start.24) | collective-permute-done | bytes 262176 | tf_op jit(solution)/shard_map/ppermute | solution.py:267
  269.9 7.5 %all-to-all-start.3 = ((f32[32,128,128]{2,1,0:T(8,128)}), f32[32,128,128]{2,1,0:T(8,128)S(1)}, u32[]{:S(2)}, u32[]{:S(2)}) async-start(f32[32,128,128]{2,1,0:T(8,128)} %bitcast.66), calls=%async_computation.3 | async-start | bytes 4194304 | tf_op jit(solution)/shard_map/all_to_all | solution.py:271
  291.4 14.8 %collective-permute-done.8.refs_3_ = f32[512,128]{1,0:T(8,128)S(1)} collective-permute-done((f32[512,128]{1,0:T(8,128)}, f32[512,128]{1,0:T(8,128)S(1)}, u32[]{:S(2)}, u32[]{:S(2)}) %collective-permute-start.8) | collective-permute-done | bytes 262176 | tf_op jit(solution)/shard_map/ppermute | solution.py:267
  306.1 9.6 %collective-permute-done.9.refs_4_ = f32[512,128]{1,0:T(8,128)S(1)} collective-permute-done((f32[512,128]{1,0:T(8,128)S(1)}, f32[512,128]{1,0:T(8,128)S(1)}, u32[]{:S(2)}, u32[]{:S(2)}) %collective-permute-start.9) | collective-permute-done | bytes 262176 | tf_op jit(solution)/shard_map/ppermute | solution.py:267
  315.8 9.6 %collective-permute-done.10.refs_5_ = f32[512,128]{1,0:T(8,128)S(1)} collective-permute-done((f32[512,128]{1,0:T(8,128)S(1)}, f32[512,128]{1,0:T(8,128)S(1)}, u32[]{:S(2)}, u32[]{:S(2)}) %collective-permute-start.10) | collective-permute-done | bytes 262176 | tf_op jit(solution)/shard_map/ppermute | solution.py:267
  328.6 5.0 %collective-permute-done.13.refs_8_ = f32[512,128]{1,0:T(8,128)} collective-permute-done((f32[512,128]{1,0:T(8,128)S(1)}, f32[512,128]{1,0:T(8,128)}, u32[]{:S(2)}, u32[]{:S(2)}) %collective-permute-start.13) | collective-permute-done | bytes 262176 | tf_op jit(solution)/shard_map/ppermute | solution.py:267
  334.9 7.6 %shard_map.84 = (f32[4096,128]{1,0:T(8,128)}, f32[4096,128]{1,0:T(8,128)}) custom-call(s32[1]{0:T(128)} %bitcast.refs_1_.refs_0_, f32[512,128]{1,0:T(8,128)} %bitcast.105, f32[512,128]{1,0:T(8,128)} %copy-done.27, f32[512,128]{1,0:T(8,128)} %copy-done.29, f32[512,128]{1,0:T(8,128)} %copy-done.31, f32[512,128]{1,0:T(8,128)} %copy-done.33, ...), custom_call_target="tpu_custom_call" | custom-call | flops 2000000000 | bytes 8388608 | tf_op jit(solution)/shard_map/pallas_call | solution.py:250
  (142 shorter events, 97.3 us)
Async XLA Ops:
  17.9 37.8 %all-to-all-start = ((f32[32,128,128]{2,1,0:T(8,128)}), f32[32,128,128]{2,1,0:T(8,128)S(1)}, u32[]{:S(2)}, u32[]{:S(2)}) async-start(f32[32,128,128]{2,1,0:T(8,128)} %bitcast.72), calls=%async_computation | async-start | bytes 4194304 | tf_op jit(solution)/shard_map/all_to_all | solution.py:271
  30.9 41.4 %collective-permute-start.2 = (f32[512,128]{1,0:T(8,128)}, f32[512,128]{1,0:T(8,128)S(1)}, u32[]{:S(2)}, u32[]{:S(2)}) collective-permute-start(f32[512,128]{1,0:T(8,128)} %get-tuple-element.40), channel_id=1, source_target_pairs={{0,17},{1,32},{16,33},{17,48},{32,49},{33,0},{48,1},{49,16},{2,19}... | collective-permute-start | bytes 786440 | tf_op jit(solution)/shard_map/ppermute | solution.py:267
  35.0 37.3 %collective-permute-start.3 = (f32[512,128]{1,0:T(8,128)}, f32[512,128]{1,0:T(8,128)S(1)}, u32[]{:S(2)}, u32[]{:S(2)}) collective-permute-start(f32[512,128]{1,0:T(8,128)} %get-tuple-element.41), channel_id=1, source_target_pairs={{0,32},{1,33},{16,48},{17,49},{32,0},{33,1},{48,16},{49,17},{2,34}... | collective-permute-start | bytes 786440 | tf_op jit(solution)/shard_map/ppermute | solution.py:267
  35.5 36.8 %collective-permute-start.4 = (f32[512,128]{1,0:T(8,128)}, f32[512,128]{1,0:T(8,128)S(1)}, u32[]{:S(2)}, u32[]{:S(2)}) collective-permute-start(f32[512,128]{1,0:T(8,128)} %get-tuple-element.42), channel_id=1, source_target_pairs={{0,33},{1,48},{16,49},{17,0},{32,1},{33,16},{48,17},{49,32},{2,35}... | collective-permute-start | bytes 786440 | tf_op jit(solution)/shard_map/ppermute | solution.py:267
  40.5 38.9 %collective-permute-start.5 = (f32[512,128]{1,0:T(8,128)}, f32[512,128]{1,0:T(8,128)}, u32[]{:S(2)}, u32[]{:S(2)}) collective-permute-start(f32[512,128]{1,0:T(8,128)} %get-tuple-element.43), channel_id=1, source_target_pairs={{0,48},{1,49},{16,0},{17,1},{32,16},{33,17},{48,32},{49,33},{2,50}... | collective-permute-start | bytes 786440 | tf_op jit(solution)/shard_map/ppermute | solution.py:267
  52.8 29.8 %collective-permute-start.6 = (f32[512,128]{1,0:T(8,128)}, f32[512,128]{1,0:T(8,128)}, u32[]{:S(2)}, u32[]{:S(2)}) collective-permute-start(f32[512,128]{1,0:T(8,128)} %get-tuple-element.44), channel_id=1, source_target_pairs={{0,49},{1,0},{16,1},{17,16},{32,17},{33,32},{48,33},{49,48},{2,51}... | collective-permute-start | bytes 786440 | tf_op jit(solution)/shard_map/ppermute | solution.py:267
  85.6 34.8 %all-to-all-start.1 = ((f32[32,128,128]{2,1,0:T(8,128)}), f32[32,128,128]{2,1,0:T(8,128)S(1)}, u32[]{:S(2)}, u32[]{:S(2)}) async-start(f32[32,128,128]{2,1,0:T(8,128)} %bitcast.67), calls=%async_computation.1 | async-start | bytes 4194304 | tf_op jit(solution)/shard_map/all_to_all | solution.py:271
  135.7 102.0 %all-to-all-start.2 = ((f32[32,128,128]{2,1,0:T(8,128)}), f32[32,128,128]{2,1,0:T(8,128)S(1)}, u32[]{:S(2)}, u32[]{:S(2)}) async-start(f32[32,128,128]{2,1,0:T(8,128)} %bitcast.69), calls=%async_computation.2 | async-start | bytes 4194304 | tf_op jit(solution)/shard_map/all_to_all | solution.py:271
  146.7 33.9 %collective-permute-start.16 = (f32[512,128]{1,0:T(8,128)S(1)}, f32[512,128]{1,0:T(8,128)S(1)}, u32[]{:S(2)}, u32[]{:S(2)}) collective-permute-start(f32[512,128]{1,0:T(8,128)S(1)} %bitcast.93), channel_id=1, source_target_pairs={{0,17},{1,32},{16,33},{17,48},{32,49},{33,0},{48,1},{49,16},{2,19}... | collective-permute-start | bytes 786440 | tf_op jit(solution)/shard_map/ppermute | solution.py:267
  147.4 43.1 %collective-permute-start.17 = (f32[512,128]{1,0:T(8,128)S(1)}, f32[512,128]{1,0:T(8,128)S(1)}, u32[]{:S(2)}, u32[]{:S(2)}) collective-permute-start(f32[512,128]{1,0:T(8,128)S(1)} %bitcast.92), channel_id=1, source_target_pairs={{0,32},{1,33},{16,48},{17,49},{32,0},{33,1},{48,16},{49,17},{2,34}... | collective-permute-start | bytes 786440 | tf_op jit(solution)/shard_map/ppermute | solution.py:267
  152.1 38.3 %collective-permute-start.18 = (f32[512,128]{1,0:T(8,128)S(1)}, f32[512,128]{1,0:T(8,128)S(1)}, u32[]{:S(2)}, u32[]{:S(2)}) collective-permute-start(f32[512,128]{1,0:T(8,128)S(1)} %bitcast.91), channel_id=1, source_target_pairs={{0,33},{1,48},{16,49},{17,0},{32,1},{33,16},{48,17},{49,32},{2,35}... | collective-permute-start | bytes 786440 | tf_op jit(solution)/shard_map/ppermute | solution.py:267
  154.6 37.9 %collective-permute-start.19 = (f32[512,128]{1,0:T(8,128)S(1)}, f32[512,128]{1,0:T(8,128)S(1)}, u32[]{:S(2)}, u32[]{:S(2)}) collective-permute-start(f32[512,128]{1,0:T(8,128)S(1)} %bitcast.90), channel_id=1, source_target_pairs={{0,48},{1,49},{16,0},{17,1},{32,16},{33,17},{48,32},{49,33},{2,50}... | collective-permute-start | bytes 786440 | tf_op jit(solution)/shard_map/ppermute | solution.py:267
  170.5 27.6 %collective-permute-start.20 = (f32[512,128]{1,0:T(8,128)S(1)}, f32[512,128]{1,0:T(8,128)S(1)}, u32[]{:S(2)}, u32[]{:S(2)}) collective-permute-start(f32[512,128]{1,0:T(8,128)S(1)} %bitcast.74), channel_id=1, source_target_pairs={{0,49},{1,0},{16,1},{17,16},{32,17},{33,32},{48,33},{49,48},{2,51}... | collective-permute-start | bytes 786440 | tf_op jit(solution)/shard_map/ppermute | solution.py:267
  215.3 34.9 %collective-permute-start.23 = (f32[512,128]{1,0:T(8,128)}, f32[512,128]{1,0:T(8,128)S(1)}, u32[]{:S(2)}, u32[]{:S(2)}) collective-permute-start(f32[512,128]{1,0:T(8,128)} %get-tuple-element.65), channel_id=1, source_target_pairs={{0,17},{1,32},{16,33},{17,48},{32,49},{33,0},{48,1},{49,16},{2,19}... | collective-permute-start | bytes 786440 | tf_op jit(solution)/shard_map/ppermute | solution.py:267
  218.9 43.0 %collective-permute-start.24 = (f32[512,128]{1,0:T(8,128)}, f32[512,128]{1,0:T(8,128)S(1)}, u32[]{:S(2)}, u32[]{:S(2)}) collective-permute-start(f32[512,128]{1,0:T(8,128)} %get-tuple-element.66), channel_id=1, source_target_pairs={{0,32},{1,33},{16,48},{17,49},{32,0},{33,1},{48,16},{49,17},{2,34}... | collective-permute-start | bytes 786440 | tf_op jit(solution)/shard_map/ppermute | solution.py:267
  220.0 41.9 %collective-permute-start.25 = (f32[512,128]{1,0:T(8,128)}, f32[512,128]{1,0:T(8,128)S(1)}, u32[]{:S(2)}, u32[]{:S(2)}) collective-permute-start(f32[512,128]{1,0:T(8,128)} %get-tuple-element.67), channel_id=1, source_target_pairs={{0,33},{1,48},{16,49},{17,0},{32,1},{33,16},{48,17},{49,32},{2,35}... | collective-permute-start | bytes 786440 | tf_op jit(solution)/shard_map/ppermute | solution.py:267
  224.4 39.1 %collective-permute-start.26 = (f32[512,128]{1,0:T(8,128)}, f32[512,128]{1,0:T(8,128)}, u32[]{:S(2)}, u32[]{:S(2)}) collective-permute-start(f32[512,128]{1,0:T(8,128)} %get-tuple-element.68), channel_id=1, source_target_pairs={{0,48},{1,49},{16,0},{17,1},{32,16},{33,17},{48,32},{49,33},{2,50}... | collective-permute-start | bytes 786440 | tf_op jit(solution)/shard_map/ppermute | solution.py:267
  237.7 29.2 %collective-permute-start.27 = (f32[512,128]{1,0:T(8,128)}, f32[512,128]{1,0:T(8,128)}, u32[]{:S(2)}, u32[]{:S(2)}) collective-permute-start(f32[512,128]{1,0:T(8,128)} %get-tuple-element.69), channel_id=1, source_target_pairs={{0,49},{1,0},{16,1},{17,16},{32,17},{33,32},{48,33},{49,48},{2,51}... | collective-permute-start | bytes 786440 | tf_op jit(solution)/shard_map/ppermute | solution.py:267
  269.9 63.7 %all-to-all-start.3 = ((f32[32,128,128]{2,1,0:T(8,128)}), f32[32,128,128]{2,1,0:T(8,128)S(1)}, u32[]{:S(2)}, u32[]{:S(2)}) async-start(f32[32,128,128]{2,1,0:T(8,128)} %bitcast.66), calls=%async_computation.3 | async-start | bytes 4194304 | tf_op jit(solution)/shard_map/all_to_all | solution.py:271
  282.1 33.7 %collective-permute-start.9 = (f32[512,128]{1,0:T(8,128)S(1)}, f32[512,128]{1,0:T(8,128)S(1)}, u32[]{:S(2)}, u32[]{:S(2)}) collective-permute-start(f32[512,128]{1,0:T(8,128)S(1)} %bitcast.99), channel_id=1, source_target_pairs={{0,17},{1,32},{16,33},{17,48},{32,49},{33,0},{48,1},{49,16},{2,19}... | collective-permute-start | bytes 786440 | tf_op jit(solution)/shard_map/ppermute | solution.py:267
  282.7 42.6 %collective-permute-start.10 = (f32[512,128]{1,0:T(8,128)S(1)}, f32[512,128]{1,0:T(8,128)S(1)}, u32[]{:S(2)}, u32[]{:S(2)}) collective-permute-start(f32[512,128]{1,0:T(8,128)S(1)} %bitcast.98), channel_id=1, source_target_pairs={{0,32},{1,33},{16,48},{17,49},{32,0},{33,1},{48,16},{49,17},{2,34}... | collective-permute-start | bytes 786440 | tf_op jit(solution)/shard_map/ppermute | solution.py:267
  287.5 37.9 %collective-permute-start.11 = (f32[512,128]{1,0:T(8,128)S(1)}, f32[512,128]{1,0:T(8,128)S(1)}, u32[]{:S(2)}, u32[]{:S(2)}) collective-permute-start(f32[512,128]{1,0:T(8,128)S(1)} %bitcast.97), channel_id=1, source_target_pairs={{0,33},{1,48},{16,49},{17,0},{32,1},{33,16},{48,17},{49,32},{2,35}... | collective-permute-start | bytes 786440 | tf_op jit(solution)/shard_map/ppermute | solution.py:267
  289.8 38.0 %collective-permute-start.12 = (f32[512,128]{1,0:T(8,128)S(1)}, f32[512,128]{1,0:T(8,128)S(1)}, u32[]{:S(2)}, u32[]{:S(2)}) collective-permute-start(f32[512,128]{1,0:T(8,128)S(1)} %bitcast.96), channel_id=1, source_target_pairs={{0,48},{1,49},{16,0},{17,1},{32,16},{33,17},{48,32},{49,33},{2,50}... | collective-permute-start | bytes 786440 | tf_op jit(solution)/shard_map/ppermute | solution.py:267
  306.1 27.4 %collective-permute-start.13 = (f32[512,128]{1,0:T(8,128)S(1)}, f32[512,128]{1,0:T(8,128)}, u32[]{:S(2)}, u32[]{:S(2)}) collective-permute-start(f32[512,128]{1,0:T(8,128)S(1)} %bitcast.76), channel_id=1, source_target_pairs={{0,49},{1,0},{16,1},{17,16},{32,17},{33,32},{48,33},{49,48},{2,51}... | collective-permute-start | bytes 786440 | tf_op jit(solution)/shard_map/ppermute | solution.py:267
  (47 other events, 766.8 us)

commit v4 on v2

v4 whole, which is shorter than its diff:
```python
import functools

import jax
import jax.numpy as jnp
from jax import lax
from jax.experimental import pallas as pl
from jax.experimental.pallas import tpu as pltpu
from jax.sharding import PartitionSpec as P

AXES = ("wide", "narrow")
QUBITS = 7
FRONT_ROWS = 64
LAST_ROWS = 64
GATE = 128
f32 = jnp.float32
bf16 = jnp.bfloat16
VMEM = pl.BlockSpec(memory_space=pltpu.VMEM)
SMEM = pl.BlockSpec(memory_space=pltpu.SMEM)


def halves(value):
    high = value.astype(bf16)
    return high, (value - high.astype(f32)).astype(bf16)


def mul(left, right):
    return jnp.dot(left, right, preferred_element_type=f32)


def pick(states, orders_ref, row):
    mapped = jnp.zeros_like(states)
    for place in range(QUBITS):
        mapped = mapped + (((states >> place) & 1) << orders_ref[row, place])
    return (mapped == lax.broadcasted_iota(jnp.int32, (GATE, GATE), 1)).astype(bf16)


def chosen(left, right, gate):
    out = []
    for part in halves(gate):
        rows = mul(left, part).astype(bf16)
        out.append(
            lax.dot_general(rows, right, (((1,), (1,)), ((), ())), preferred_element_type=f32)
            .astype(bf16)
        )
    return out


def unit_turn(quarters):
    whole = jnp.floor(quarters + 0.5)
    r = (quarters - whole) * 1.5707963267948966
    s = r * r
    sine = r + r * s * (-1.6666654611e-1 + s * (8.3321608736e-3 - s * 1.9515295891e-4))
    cosine = 1.0 - 0.5 * s + s * s * (
        4.166664568298827e-2 + s * (-1.388731625493765e-3 + s * 2.443315711809948e-5)
    )
    quarter = whole.astype(jnp.int32)
    swap = (quarter & 1) == 1
    base_sin = jnp.where(swap, cosine, sine)
    base_cos = jnp.where(swap, sine, cosine)
    sine = jnp.where((quarter & 2) == 2, -base_sin, base_sin)
    cosine = jnp.where(((quarter + 1) & 2) == 2, -base_cos, base_cos)
    return cosine, sine


def front_kernel(base_ref, orders_ref, masks_ref, angles_ref, real_ref, imag_ref, gates_ref,
                 send_ref, high_ref, low_ref, need_ref, angle_ref):
    top, count = real_ref.shape[:2]
    pairs = masks_ref.shape[0]
    step = pl.program_id(0)

    @pl.when(step == 0)
    def _():
        states = lax.broadcasted_iota(jnp.int32, (GATE, GATE), 0)
        one_hot = pick(states, orders_ref, 0)
        real_high, real_low = chosen(one_hot, one_hot, gates_ref[0, 0])
        imag_high, imag_low = chosen(one_hot, one_hot, gates_ref[0, 1])
        for ref, real, imag in ((high_ref, real_high, imag_high), (low_ref, real_low, imag_low)):
            ref[:GATE, :GATE] = real
            ref[:GATE, GATE:] = -imag
            ref[GATE:, :GATE] = imag
            ref[GATE:, GATE:] = real
        lane = lax.broadcasted_iota(jnp.int32, (8, GATE), 1)
        column = lax.broadcasted_iota(jnp.int32, (GATE, GATE), 1)
        row = lax.broadcasted_iota(jnp.int32, (GATE, GATE), 0)
        need = jnp.zeros((8, GATE), jnp.int32) - 1
        values = jnp.zeros((GATE, GATE), f32)
        for pair in range(pairs):
            mask = masks_ref[pair, 0] | masks_ref[pair, 1]
            inside = mask & (GATE - 1)
            quarters = jnp.full((GATE, GATE), angles_ref[pair] * 0.6366197723675814, f32)
            held = jnp.where((column & inside) == inside, quarters, 0.0)
            for part in range(3):
                spot = part * pairs + pair
                need = jnp.where(lane == spot, mask & ~(GATE - 1), need)
                piece = held.astype(bf16).astype(f32)
                values = jnp.where(row == spot, piece, values)
                held = held - piece
        need_ref[...] = need
        angle_ref[...] = values.astype(bf16)

    def turned(left, right):
        return lax.dot_general(left, right, (((1,), (1,)), ((), ())), preferred_element_type=f32)

    rows = top * count
    both = jnp.concatenate(
        [real_ref[...].reshape(rows, GATE), imag_ref[...].reshape(rows, GATE)], axis=1
    )
    x_high, x_low = halves(both)
    new = (
        turned(x_high, high_ref[...])
        + turned(x_high, low_ref[...])
        + turned(x_low, high_ref[...])
    )
    shape = (top, count, GATE)
    flat = (
        lax.broadcasted_iota(jnp.int32, shape, 0) * (256 * GATE)
        + lax.broadcasted_iota(jnp.int32, shape, 1) * GATE
        + (base_ref[0] + step * (count * GATE))
    ).reshape(rows, GATE)
    need = need_ref[0:1, :]
    conditions = jnp.where((flat & need) == need, 1.0, 0.0).astype(bf16)
    cosine, sine = unit_turn(mul(conditions, angle_ref[...]))
    real = new[:, :GATE]
    imag = new[:, GATE:]
    for part, value in enumerate((real * cosine - imag * sine, real * sine + imag * cosine)):
        send_ref[:, part] = jnp.transpose(value.reshape(shape), (1, 0, 2))


def middle_kernel(second_ref, third_ref, got_ref, back_ref, mid_ref, high_ref, low_ref):
    step = pl.program_id(0)
    inputs = got_ref.shape[0]

    @pl.when(step == 0)
    def _():
        high_ref[0], low_ref[0] = halves(second_ref[...])
        high_ref[1], low_ref[1] = halves(third_ref[...])

    def apply(which, x):
        x_high, x_low = halves(x)
        high = high_ref[which]
        return mul(high, x_high) + mul(low_ref[which], x_high) + mul(high, x_low)

    @pl.when(step < 8)
    def _():
        parts = [jnp.transpose(got_ref[:, 0, part], (1, 0, 2)) for part in range(2)]
        columns = [
            jnp.concatenate([part[inner * 4 + rest] for part in parts for inner in range(4)], axis=0)
            for rest in range(4)
        ]
        out = apply(0, jnp.concatenate(columns, axis=1))
        for part in range(2):
            stack = jnp.stack(
                [
                    out[
                        part * GATE + inner * inputs : part * GATE + (inner + 1) * inputs,
                        rest * GATE : (rest + 1) * GATE,
                    ]
                    for rest in range(4)
                    for inner in range(4)
                ],
                axis=0,
            )
            mid_ref[part, :, step] = jnp.transpose(stack, (1, 0, 2))

    @pl.when(step >= 8)
    def _():
        count = back_ref.shape[0]
        first = (step - 8) * count
        columns = [
            jnp.concatenate(
                [mid_ref[part, first + wide].reshape(GATE, GATE) for part in range(2)], axis=0
            )
            for wide in range(count)
        ]
        out = apply(1, jnp.concatenate(columns, axis=1))
        for wide in range(count):
            back_ref[wide] = out[:, wide * GATE : (wide + 1) * GATE].reshape(8, 2, 16, GATE)


def last_kernel(got_ref, real_ref, imag_ref):
    for part, ref in enumerate((real_ref, imag_ref)):
        ref[...] = jnp.transpose(got_ref[:, part], (1, 0, 2))


def ordered(gate_pair, order_row, row_states, column_states):
    def one_hot(states):
        places = jnp.arange(QUBITS, dtype=jnp.int32)
        digits = states[:, None] >> places[None, :] & 1
        mapped = jnp.sum(digits << order_row[None, :], axis=1)
        return (mapped[:, None] == jnp.arange(GATE, dtype=jnp.int32)[None, :]).astype(f32)

    precise = lax.Precision.HIGHEST
    left, right = one_hot(row_states), one_hot(column_states)
    return [
        jnp.dot(jnp.dot(left, part, precision=precise), right.T, precision=precise)
        for part in (gate_pair[0], gate_pair[1])
    ]


def body(state_real, state_imag, gates, gate_orders, phase_masks, phase_angles):
    real_part = state_real[0, 0]
    imag_part = state_imag[0, 0]
    rows, columns = real_part.shape
    wide_count = lax.axis_size("wide")
    narrow_count = lax.axis_size("narrow")
    devices = wide_count * narrow_count
    base = (lax.axis_index("narrow") * wide_count + lax.axis_index("wide")) * (rows * columns)
    packed = jax.ShapeDtypeStruct((devices, 2, 16, columns), f32)
    tall = jax.ShapeDtypeStruct((16, devices, columns), f32)
    count = FRONT_ROWS
    piece = pl.BlockSpec((16, count, columns), lambda i: (0, i, 0))
    send = pl.pallas_call(
        front_kernel,
        out_shape=packed,
        grid=(devices // count,),
        in_specs=[SMEM] * 4 + [piece, piece, VMEM],
        out_specs=pl.BlockSpec((count, 2, 16, columns), lambda i: (i, 0, 0, 0)),
        scratch_shapes=[
            pltpu.VMEM((256, 256), bf16),
            pltpu.VMEM((256, 256), bf16),
            pltpu.VMEM((8, GATE), jnp.int32),
            pltpu.VMEM((GATE, GATE), bf16),
        ],
        name="front",
    )(
        base[None],
        gate_orders,
        phase_masks,
        phase_angles,
        real_part.reshape(16, devices, columns),
        imag_part.reshape(16, devices, columns),
        gates,
    )

    def exchange(block):
        return lax.all_to_all(block, AXES, split_axis=0, concat_axis=0, tiled=True)

    got = exchange(send)
    states = jnp.arange(GATE, dtype=jnp.int32)
    by_inner = states % 32 * 4 + states // 32
    second = ordered(gates[1], gate_orders[1], by_inner, by_inner)
    swapped = states // 16 * 16 + states % 4 * 4 + states // 4 % 4
    third = ordered(gates[2], gate_orders[2], states, swapped)
    second = jnp.concatenate(
        [
            jnp.concatenate([second[0], -second[1]], axis=1),
            jnp.concatenate([second[1], second[0]], axis=1),
        ],
        axis=0,
    )
    third = jnp.stack(
        [
            jnp.concatenate([third[0], -third[1]], axis=1).reshape(8, 16, 256),
            jnp.concatenate([third[1], third[0]], axis=1).reshape(8, 16, 256),
        ],
        axis=1,
    ).reshape(256, 256)
    back = pl.pallas_call(
        middle_kernel,
        out_shape=jax.ShapeDtypeStruct((wide_count, narrow_count, 2, 16, columns), f32),
        grid=(16,),
        in_specs=[
            VMEM,
            VMEM,
            pl.BlockSpec(
                (wide_count, 1, 2, 16, columns), lambda i: (0, jnp.minimum(i, 7), 0, 0, 0)
            ),
        ],
        out_specs=pl.BlockSpec(
            (wide_count // 8, narrow_count, 2, 16, columns),
            lambda i: (jnp.maximum(i - 8, 0), 0, 0, 0, 0),
        ),
        scratch_shapes=[
            pltpu.VMEM((2, wide_count, narrow_count, 16, columns), f32),
            pltpu.VMEM((2, 256, 256), bf16),
            pltpu.VMEM((2, 256, 256), bf16),
        ],
        name="middle",
    )(second, third, got.reshape(wide_count, narrow_count, 2, 16, columns))
    final = exchange(back.reshape(devices, 2, 16, columns))
    count = LAST_ROWS
    piece = pl.BlockSpec((16, count, columns), lambda i: (0, i, 0))
    out_real, out_imag = pl.pallas_call(
        last_kernel,
        out_shape=(tall, tall),
        grid=(devices // count,),
        in_specs=[pl.BlockSpec((count, 2, 16, columns), lambda i: (i, 0, 0, 0))],
        out_specs=(piece, piece),
        name="last",
    )(final)
    out_real, out_imag = out_real.reshape(rows, columns), out_imag.reshape(rows, columns)
    return (out_real[None, None], out_imag[None, None])


def solution(mesh):
    placed = (P("narrow", "wide", None, None), P("narrow", "wide", None, None), P(), P(), P(), P())
    return jax.shard_map(
        body,
        mesh=mesh,
        in_specs=placed,
        out_specs=(P("narrow", "wide", None, None), P("narrow", "wide", None, None)),
        check_vma=False,
    )
```

time: 263 us -> 248 us (0.943)
  Pallas kernels: 41.7 us -> 26.4 us
    pallas_call x3, Pallas kernels: 41.7 us -> 26.4 us  [the longest x1 12.5 us: body(): pl.pallas_call(middle_kernel, out_shape=jax.ShapeDtypeStruct((wide_count,...]
  transfers between devices with their start and end apart: 1 -> 1, of which waited for: 1 -> 1; matrix products, arithmetic and copies ran while one was open for 1% -> 2% of each run, Pallas kernels for 0% -> 0%
where the time goes in v4:
time: 248 us; the launch traced here: 246 us
  blocking collectives  105 us (42%)
  waiting for transfers between devices  92.4 us (37%)
  Pallas kernels  26.4 us (11%)
  starting transfers between devices  15.7 us (6%)
    all_to_all x1, blocking collectives, exchange(): return lax.all_to_all(block, AXES, split_axis=0, concat_axis=0, tiled=True)  105 us
    all_to_all x1, waiting for transfers between devices, exchange(): return lax.all_to_all(block, AXES, split_axis=0, concat_axis=0, tiled=True)  92.4 us
    all_to_all x1, starting transfers between devices, exchange(): return lax.all_to_all(block, AXES, split_axis=0, concat_axis=0, tiled=True)  15.7 us
    pallas_call x1, Pallas kernels, body(): pl.pallas_call(middle_kernel, out_shape=jax.ShapeDtypeStruct((wide_count,...  12.5 us
    pallas_call x1, Pallas kernels, body(): pl.pallas_call(front_kernel, out_shape=packed, grid=(devices // count,),...  8.91 us
    pallas_call x1, Pallas kernels, body(): pl.pallas_call(last_kernel, out_shape=(tall, tall), grid=(devices // coun...  5.01 us
  transfers between devices with their start and end apart: 1, of which 1 were waited for; matrix products, arithmetic and copies ran while one was open for 2% of the time, Pallas kernels for 0%

profile of v4, /device:TPU:2, one launch (start us, length us, event | category | flops | bytes accessed | tf_op | source)
XLA Modules:
  0.0 245.7 jit_solution(16515499431532689210)
XLA Ops:
  0.6 1.3 copy.30.masks_ref
  2.0 8.9 %front.1 = f32[256,2,16,128]{3,2,1,0:T(8,128)} custom-call(s32[1]{0:T(128)} %bitcast.9.base_ref, s32[3,7]{1,0:T(4,128)} %orders_ref.1, s32[8,2]{1,0:T(8,128)} %copy.30.masks_ref, f32[8]{0:T(128)} %angles_ref.1, f32[16,256,128]{2,1,0:T(8,128)} %bitcast.31, f32[16,256,128]{2,1,0:T(8,128)} %bitcast.32, f32[3,2,128,128]{3,2,1,0:T(8,128)} %gates_ref.1), custom_call_target="tpu_custom_call" | custom-call | tf_op jit(solution)/shard_map/front/pallas_call | solution.py:212
  10.9 0.0 copy-start.1
  10.9 0.0 copy-start
  10.9 15.7 %all-to-all-start = ((f32[256,2,16,128]{3,2,1,0:T(8,128)}), f32[256,2,16,128]{3,2,1,0:T(8,128)}, u32[]{:S(2)}, u32[]{:S(2)}) async-start(f32[256,2,16,128]{3,2,1,0:T(8,128)} %front.1), calls=%async_computation | async-start | bytes 8388608 | tf_op jit(solution)/shard_map/all_to_all | solution.py:236
  26.6 0.0 copy-done.1
  26.6 0.1 shift-left_reduce_fusion
  26.7 0.0 copy-done
  26.7 0.2 fusion
  27.0 0.2 fusion.2
  27.2 0.2 fusion.10
  27.5 0.2 fusion.33
  27.7 0.1 copy.27
  27.8 0.1 copy.28
  28.0 0.7 copy.29
  28.7 0.2 fusion.4
  28.9 0.2 fusion.6
  29.2 0.3 fusion.15
  29.5 0.3 fusion.32
  29.7 0.7 maximum_maximum_fusion.second_ref
  30.5 92.4 %all-to-all-done = f32[256,2,16,128]{3,2,1,0:T(8,128)} async-done(((f32[256,2,16,128]{3,2,1,0:T(8,128)}), f32[256,2,16,128]{3,2,1,0:T(8,128)}, u32[]{:S(2)}, u32[]{:S(2)}) %all-to-all-start) | async-done | bytes 4194336 | tf_op jit(solution)/shard_map/all_to_all | solution.py:236
  122.9 12.5 %middle.1 = f32[32,8,2,16,128]{4,3,2,1,0:T(8,128)} custom-call(f32[256,256]{1,0:T(8,128)} %maximum_maximum_fusion.second_ref, f32[256,256]{1,0:T(8,128)} %bitcast.33, f32[32,8,2,16,128]{4,3,2,1,0:T(8,128)} %bitcast.12.got_ref), custom_call_target="tpu_custom_call" | custom-call | tf_op jit(solution)/shard_map/middle/pallas_call | solution.py:258
  135.4 105.3 %all_to_all.10.got_ref = f32[256,2,16,128]{3,2,1,0:T(8,128)} all-to-all(f32[256,2,16,128]{3,2,1,0:T(8,128)} %bitcast.30), channel_id=1, replica_groups=mesh['wide'=32,'narrow'=8] {'wide','narrow'}, dimensions={0} | all-to-all | bytes 8388608 | tf_op jit(solution)/shard_map/all_to_all | solution.py:236
  240.7 5.0 %last.1 = (f32[16,256,128]{2,1,0:T(8,128)}, f32[16,256,128]{2,1,0:T(8,128)}) custom-call(f32[256,2,16,128]{3,2,1,0:T(8,128)} %all_to_all.10.got_ref), custom_call_target="tpu_custom_call" | custom-call | tf_op jit(solution)/shard_map/last/pallas_call | solution.py:283
  (5 shorter events, 0.1 us)
Async XLA Ops:
  10.9 15.7 %copy-start.1 = (s32[3,7]{1,0:T(4,128)S(1)}, s32[3,7]{1,0:T(4,128)}, u32[]{:S(2)}) copy-start(s32[3,7]{1,0:T(4,128)} %orders_ref.1) | copy-start | bytes 256
  10.9 15.8 %copy-start = (f32[3,2,128,128]{3,2,1,0:T(8,128)S(1)}, f32[3,2,128,128]{3,2,1,0:T(8,128)}, u32[]{:S(2)}) copy-start(f32[3,2,128,128]{3,2,1,0:T(8,128)} %gates_ref.1) | copy-start | bytes 1179652
  10.9 112.0 %all-to-all-start = ((f32[256,2,16,128]{3,2,1,0:T(8,128)}), f32[256,2,16,128]{3,2,1,0:T(8,128)}, u32[]{:S(2)}, u32[]{:S(2)}) async-start(f32[256,2,16,128]{3,2,1,0:T(8,128)} %front.1), calls=%async_computation | async-start | bytes 8388608 | tf_op jit(solution)/shard_map/all_to_all | solution.py:236

commit v5 on v4

--- a/solution.py
+++ b/solution.py
@@ -10,7 +10,8 @@
 AXES = ("wide", "narrow")
 QUBITS = 7
 FRONT_ROWS = 64
-LAST_ROWS = 64
+LAST_ROWS = 128
+GATE_STEPS = 2
 GATE = 128
 f32 = jnp.float32
 bf16 = jnp.bfloat16
@@ -63,10 +64,13 @@
 
 
 def front_kernel(base_ref, orders_ref, masks_ref, angles_ref, real_ref, imag_ref, gates_ref,
-                 send_ref, high_ref, low_ref, need_ref, angle_ref):
+                 send_ref, gate_ref, need_ref, weight_ref, table_ref, place_ref):
     top, count = real_ref.shape[:2]
-    pairs = masks_ref.shape[0]
+    pairs = masks_ref.shape[1]
+    patterns = 2**pairs
+    rows = top * count
     step = pl.program_id(0)
+    order = range(top)
 
     @pl.when(step == 0)
     def _():
@@ -74,107 +78,128 @@
         one_hot = pick(states, orders_ref, 0)
         real_high, real_low = chosen(one_hot, one_hot, gates_ref[0, 0])
         imag_high, imag_low = chosen(one_hot, one_hot, gates_ref[0, 1])
-        for ref, real, imag in ((high_ref, real_high, imag_high), (low_ref, real_low, imag_low)):
-            ref[:GATE, :GATE] = real
-            ref[:GATE, GATE:] = -imag
-            ref[GATE:, :GATE] = imag
-            ref[GATE:, GATE:] = real
+        for spot, real, imag in (
+            (0, real_high, imag_high),
+            (2, real_low, imag_low),
+            (4, real_high, imag_high),
+        ):
+            left = slice(spot * GATE, (spot + 1) * GATE)
+            right = slice((spot + 1) * GATE, (spot + 2) * GATE)
+            gate_ref[:GATE, left] = real
+            gate_ref[:GATE, right] = -imag
+            gate_ref[GATE:, left] = imag
+            gate_ref[GATE:, right] = real
         lane = lax.broadcasted_iota(jnp.int32, (8, GATE), 1)
-        column = lax.broadcasted_iota(jnp.int32, (GATE, GATE), 1)
-        row = lax.broadcasted_iota(jnp.int32, (GATE, GATE), 0)
+        spot = lax.broadcasted_iota(jnp.int32, (GATE, GATE), 0)
+        column = lax.broadcasted_iota(jnp.int32, (patterns, GATE), 1)
+        pattern = lax.broadcasted_iota(jnp.int32, (patterns, GATE), 0)
         need = jnp.zeros((8, GATE), jnp.int32) - 1
-        values = jnp.zeros((GATE, GATE), f32)
+        weight = jnp.zeros((GATE, GATE), f32)
+        quarters = jnp.zeros((patterns, GATE), f32)
         for pair in range(pairs):
-            mask = masks_ref[pair, 0] | masks_ref[pair, 1]
+            mask = masks_ref[0, pair] | masks_ref[1, pair]
             inside = mask & (GATE - 1)
-            quarters = jnp.full((GATE, GATE), angles_ref[pair] * 0.6366197723675814, f32)
-            held = jnp.where((column & inside) == inside, quarters, 0.0)
-            for part in range(3):
-                spot = part * pairs + pair
-                need = jnp.where(lane == spot, mask & ~(GATE - 1), need)
-                piece = held.astype(bf16).astype(f32)
-                values = jnp.where(row == spot, piece, values)
-                held = held - piece
+            need = jnp.where(lane == pair, mask & ~(GATE - 1), need)
+            weight = jnp.where(spot == pair, float(2**pair), weight)
+            met = ((column & inside) == inside) & (((pattern >> pair) & 1) == 1)
+            quarters = quarters + jnp.where(met, angles_ref[pair] * 0.6366197723675814, 0.0)
         need_ref[...] = need
-        angle_ref[...] = values.astype(bf16)
-
-    def turned(left, right):
-        return lax.dot_general(left, right, (((1,), (1,)), ((), ())), preferred_element_type=f32)
-
-    rows = top * count
+        weight_ref[...] = weight.astype(bf16)
+        for half, value in enumerate(unit_turn(quarters)):
+            lanes = slice(half * GATE, (half + 1) * GATE)
+            table_ref[:patterns, lanes], table_ref[patterns:, lanes] = halves(value)
+        within = lax.broadcasted_iota(jnp.int32, (count, GATE), 0) * GATE
+        for spot, high in enumerate(order):
+            place_ref[spot] = within + (base_ref[0] + high * (256 * GATE))
+
     both = jnp.concatenate(
-        [real_ref[...].reshape(rows, GATE), imag_ref[...].reshape(rows, GATE)], axis=1
+        [
+            jnp.concatenate([ref[high] for high in order], axis=0)
+            for ref in (real_ref, imag_ref)
+        ],
+        axis=1,
     )
     x_high, x_low = halves(both)
-    new = (
-        turned(x_high, high_ref[...])
-        + turned(x_high, low_ref[...])
-        + turned(x_low, high_ref[...])
-    )
-    shape = (top, count, GATE)
-    flat = (
-        lax.broadcasted_iota(jnp.int32, shape, 0) * (256 * GATE)
-        + lax.broadcasted_iota(jnp.int32, shape, 1) * GATE
-        + (base_ref[0] + step * (count * GATE))
-    ).reshape(rows, GATE)
+    new = lax.dot_general(
+        jnp.concatenate([x_high, x_high, x_low], axis=1),
+        gate_ref[...],
+        (((1,), (1,)), ((), ())),
+        preferred_element_type=f32,
+    )
+    flat = place_ref[...].reshape(rows, GATE) + step * (count * GATE)
     need = need_ref[0:1, :]
     conditions = jnp.where((flat & need) == need, 1.0, 0.0).astype(bf16)
-    cosine, sine = unit_turn(mul(conditions, angle_ref[...]))
+    found = mul(conditions, weight_ref[...])
+    lane = lax.broadcasted_iota(jnp.int32, (rows, GATE), 1).astype(f32)
+    chosen_rows = [
+        jnp.where(found == lane + float(first), 1.0, 0.0).astype(bf16)
+        for first in range(0, patterns, GATE)
+    ]
+    turn = mul(jnp.concatenate(chosen_rows * 2, axis=1), table_ref[...])
+    cosine, sine = turn[:, :GATE], turn[:, GATE:]
     real = new[:, :GATE]
     imag = new[:, GATE:]
     for part, value in enumerate((real * cosine - imag * sine, real * sine + imag * cosine)):
-        send_ref[:, part] = jnp.transpose(value.reshape(shape), (1, 0, 2))
-
-
-def middle_kernel(second_ref, third_ref, got_ref, back_ref, mid_ref, high_ref, low_ref):
+        send_ref[:, part] = jnp.transpose(value.reshape(top, count, GATE), (1, 0, 2))
+
+
+def middle_kernel(second_ref, third_ref, got_ref, back_ref, mid_ref, gates_ref):
     step = pl.program_id(0)
-    inputs = got_ref.shape[0]
+    inputs, together = got_ref.shape[:2]
+    steps = 8 // together
 
     @pl.when(step == 0)
     def _():
-        high_ref[0], low_ref[0] = halves(second_ref[...])
-        high_ref[1], low_ref[1] = halves(third_ref[...])
+        for which, ref in enumerate((second_ref, third_ref)):
+            high, low = halves(ref[...])
+            gates_ref[which] = jnp.concatenate([high, low, high], axis=1)
 
     def apply(which, x):
         x_high, x_low = halves(x)
-        high = high_ref[which]
-        return mul(high, x_high) + mul(low_ref[which], x_high) + mul(high, x_low)
-
-    @pl.when(step < 8)
+        return mul(gates_ref[which], jnp.concatenate([x_high, x_high, x_low], axis=0))
+
+    @pl.when(step < steps)
     def _():
-        parts = [jnp.transpose(got_ref[:, 0, part], (1, 0, 2)) for part in range(2)]
-        columns = [
-            jnp.concatenate([part[inner * 4 + rest] for part in parts for inner in range(4)], axis=0)
-            for rest in range(4)
-        ]
-        out = apply(0, jnp.concatenate(columns, axis=1))
-        for part in range(2):
-            stack = jnp.stack(
-                [
-                    out[
-                        part * GATE + inner * inputs : part * GATE + (inner + 1) * inputs,
-                        rest * GATE : (rest + 1) * GATE,
-                    ]
-                    for rest in range(4)
-                    for inner in range(4)
-                ],
-                axis=0,
-            )
-            mid_ref[part, :, step] = jnp.transpose(stack, (1, 0, 2))
-
-    @pl.when(step >= 8)
+        for narrow in range(together):
+            parts = [jnp.transpose(got_ref[:, narrow, part], (1, 0, 2)) for part in range(2)]
+            columns = [
+                jnp.concatenate(
+                    [part[inner * 4 + rest] for part in parts for inner in range(4)], axis=0
+                )
+                for rest in range(4)
+            ]
+            out = apply(0, jnp.concatenate(columns, axis=1))
+            for part in range(2):
+                stack = jnp.stack(
+                    [
+                        out[
+                            part * GATE + inner * inputs : part * GATE + (inner + 1) * inputs,
+                            rest * GATE : (rest + 1) * GATE,
+                        ]
+                        for rest in range(4)
+                        for inner in range(4)
+                    ],
+                    axis=0,
+                )
+                mid_ref[part, :, step * together + narrow] = jnp.transpose(stack, (1, 0, 2))
+
+    @pl.when(step >= steps)
     def _():
         count = back_ref.shape[0]
-        first = (step - 8) * count
-        columns = [
-            jnp.concatenate(
-                [mid_ref[part, first + wide].reshape(GATE, GATE) for part in range(2)], axis=0
-            )
-            for wide in range(count)
-        ]
-        out = apply(1, jnp.concatenate(columns, axis=1))
-        for wide in range(count):
-            back_ref[wide] = out[:, wide * GATE : (wide + 1) * GATE].reshape(8, 2, 16, GATE)
+
+        for group in range(count // 4):
+            first = (step - steps) * count + group * 4
+            columns = [
+                jnp.concatenate(
+                    [mid_ref[part, first + wide].reshape(GATE, GATE) for part in range(2)], axis=0
+                )
+                for wide in range(4)
+            ]
+            out = apply(1, jnp.concatenate(columns, axis=1))
+            for wide in range(4):
+                back_ref[group * 4 + wide] = out[:, wide * GATE : (wide + 1) * GATE].reshape(
+                    8, 2, 16, GATE
+                )
 
 
 def last_kernel(got_ref, real_ref, imag_ref):
@@ -216,16 +241,17 @@
         in_specs=[SMEM] * 4 + [piece, piece, VMEM],
         out_specs=pl.BlockSpec((count, 2, 16, columns), lambda i: (i, 0, 0, 0)),
         scratch_shapes=[
-            pltpu.VMEM((256, 256), bf16),
-            pltpu.VMEM((256, 256), bf16),
+            pltpu.VMEM((256, 768), bf16),
             pltpu.VMEM((8, GATE), jnp.int32),
             pltpu.VMEM((GATE, GATE), bf16),
+            pltpu.VMEM((2 * 2 ** phase_masks.shape[0], 256), bf16),
+            pltpu.VMEM((16, count, GATE), jnp.int32),
         ],
         name="front",
     )(
         base[None],
         gate_orders,
-        phase_masks,
+        phase_masks.T,
         phase_angles,
         real_part.reshape(16, devices, columns),
         imag_part.reshape(16, devices, columns),
@@ -258,22 +284,22 @@
     back = pl.pallas_call(
         middle_kernel,
         out_shape=jax.ShapeDtypeStruct((wide_count, narrow_count, 2, 16, columns), f32),
-        grid=(16,),
+        grid=(GATE_STEPS * 2,),
         in_specs=[
             VMEM,
             VMEM,
             pl.BlockSpec(
-                (wide_count, 1, 2, 16, columns), lambda i: (0, jnp.minimum(i, 7), 0, 0, 0)
+                (wide_count, narrow_count // GATE_STEPS, 2, 16, columns),
+                lambda i: (0, jnp.minimum(i, GATE_STEPS - 1), 0, 0, 0),
             ),
         ],
         out_specs=pl.BlockSpec(
-            (wide_count // 8, narrow_count, 2, 16, columns),
-            lambda i: (jnp.maximum(i - 8, 0), 0, 0, 0, 0),
+            (wide_count // GATE_STEPS, narrow_count, 2, 16, columns),
+            lambda i: (jnp.maximum(i - GATE_STEPS, 0), 0, 0, 0, 0),
         ),
         scratch_shapes=[
             pltpu.VMEM((2, wide_count, narrow_count, 16, columns), f32),
-            pltpu.VMEM((2, 256, 256), bf16),
-            pltpu.VMEM((2, 256, 256), bf16),
+            pltpu.VMEM((2, 256, 768), bf16),
         ],
         name="middle",
     )(second, third, got.reshape(wide_count, narrow_count, 2, 16, columns))

time: 248 us -> 241 us (0.972)
  Pallas kernels: 26.4 us -> 20.5 us
    pallas_call x1, Pallas kernels: 12.5 us -> 8.07 us  [body(): pl.pallas_call(middle_kernel, out_shape=jax.ShapeDtypeStruct((wide_count,...]
where the time goes in v5:
time: 241 us; the launch traced here: 238 us
  blocking collectives  105 us (44%)
  waiting for transfers between devices  92.4 us (38%)
  Pallas kernels  20.5 us (9%)
  starting transfers between devices  15.7 us (7%)
    all_to_all x1, blocking collectives, exchange(): return lax.all_to_all(block, AXES, split_axis=0, concat_axis=0, tiled=True)  105 us
    all_to_all x1, waiting for transfers between devices, exchange(): return lax.all_to_all(block, AXES, split_axis=0, concat_axis=0, tiled=True)  92.4 us
    all_to_all x1, starting transfers between devices, exchange(): return lax.all_to_all(block, AXES, split_axis=0, concat_axis=0, tiled=True)  15.7 us
    pallas_call x1, Pallas kernels, body(): pl.pallas_call(front_kernel, out_shape=packed, grid=(devices // count,),...  8.31 us
    pallas_call x1, Pallas kernels, body(): pl.pallas_call(middle_kernel, out_shape=jax.ShapeDtypeStruct((wide_count,...  8.07 us
  transfers between devices with their start and end apart: 1, of which 1 were waited for; matrix products, arithmetic and copies ran while one was open for 2% of the time, Pallas kernels for 0%

profile of v5, /device:TPU:2, one launch (start us, length us, event | category | flops | bytes accessed | tf_op | source)
XLA Modules:
  0.0 238.5 jit_solution(3038469961711057261)
XLA Ops:
  0.6 8.3 %front.1 = f32[256,2,16,128]{3,2,1,0:T(8,128)} custom-call(s32[1]{0:T(128)} %bitcast.9.base_ref, s32[3,7]{1,0:T(4,128)} %orders_ref.1, s32[2,8]{1,0:T(2,128)} %bitcast.37, f32[8]{0:T(128)} %angles_ref.1, f32[16,256,128]{2,1,0:T(8,128)} %bitcast.32, f32[16,256,128]{2,1,0:T(8,128)} %bitcast.33, f32[3,2,128,128]{3,2,1,0:T(8,128)} %gates_ref.1), custom_call_target="tpu_custom_call" | custom-call | tf_op jit(solution)/shard_map/front/pallas_call | solution.py:237
  8.9 0.0 copy-start.1
  9.0 0.0 copy-start
  9.0 15.7 %all-to-all-start = ((f32[256,2,16,128]{3,2,1,0:T(8,128)}), f32[256,2,16,128]{3,2,1,0:T(8,128)}, u32[]{:S(2)}, u32[]{:S(2)}) async-start(f32[256,2,16,128]{3,2,1,0:T(8,128)} %front.1), calls=%async_computation | async-start | bytes 8388608 | tf_op jit(solution)/shard_map/all_to_all | solution.py:262
  24.7 0.0 copy-done.1
  24.7 0.1 shift-left_reduce_fusion
  24.8 0.0 copy-done
  24.8 0.2 fusion
  25.0 0.2 fusion.2
  25.3 0.2 fusion.10
  25.5 0.2 fusion.33
  25.8 0.1 copy.25
  25.9 0.1 copy.26
  26.0 0.7 copy.27
  26.7 0.2 fusion.4
  27.0 0.2 fusion.6
  27.2 0.3 fusion.15
  27.5 0.3 fusion.32
  27.8 0.7 maximum_maximum_fusion.second_ref
  28.5 92.4 %all-to-all-done = f32[256,2,16,128]{3,2,1,0:T(8,128)} async-done(((f32[256,2,16,128]{3,2,1,0:T(8,128)}), f32[256,2,16,128]{3,2,1,0:T(8,128)}, u32[]{:S(2)}, u32[]{:S(2)}) %all-to-all-start) | async-done | bytes 4194336 | tf_op jit(solution)/shard_map/all_to_all | solution.py:262
  120.9 8.1 %middle.1 = f32[32,8,2,16,128]{4,3,2,1,0:T(8,128)} custom-call(f32[256,256]{1,0:T(8,128)} %maximum_maximum_fusion.second_ref, f32[256,256]{1,0:T(8,128)} %bitcast.34, f32[32,8,2,16,128]{4,3,2,1,0:T(8,128)} %bitcast.13.got_ref), custom_call_target="tpu_custom_call" | custom-call | tf_op jit(solution)/shard_map/middle/pallas_call | solution.py:284
  129.0 105.3 %all_to_all.10.got_ref = f32[256,2,16,128]{3,2,1,0:T(8,128)} all-to-all(f32[256,2,16,128]{3,2,1,0:T(8,128)} %bitcast.31), channel_id=1, replica_groups=mesh['wide'=32,'narrow'=8] {'wide','narrow'}, dimensions={0} | all-to-all | bytes 8388608 | tf_op jit(solution)/shard_map/all_to_all | solution.py:262
  234.4 4.1 %last.1 = (f32[16,256,128]{2,1,0:T(8,128)}, f32[16,256,128]{2,1,0:T(8,128)}) custom-call(f32[256,2,16,128]{3,2,1,0:T(8,128)} %all_to_all.10.got_ref), custom_call_target="tpu_custom_call" | custom-call | tf_op jit(solution)/shard_map/last/pallas_call | solution.py:309
  (5 shorter events, 0.1 us)
Async XLA Ops:
  8.9 15.7 %copy-start.1 = (s32[3,7]{1,0:T(4,128)S(1)}, s32[3,7]{1,0:T(4,128)}, u32[]{:S(2)}) copy-start(s32[3,7]{1,0:T(4,128)} %orders_ref.1) | copy-start | bytes 256
  9.0 15.8 %copy-start = (f32[3,2,128,128]{3,2,1,0:T(8,128)S(1)}, f32[3,2,128,128]{3,2,1,0:T(8,128)}, u32[]{:S(2)}) copy-start(f32[3,2,128,128]{3,2,1,0:T(8,128)} %gates_ref.1) | copy-start | bytes 1179652
  9.0 112.0 %all-to-all-start = ((f32[256,2,16,128]{3,2,1,0:T(8,128)}), f32[256,2,16,128]{3,2,1,0:T(8,128)}, u32[]{:S(2)}, u32[]{:S(2)}) async-start(f32[256,2,16,128]{3,2,1,0:T(8,128)} %front.1), calls=%async_computation | async-start | bytes 8388608 | tf_op jit(solution)/shard_map/all_to_all | solution.py:262

commit v6 on v4

v6 whole, which is shorter than its diff:
```python
import functools

import jax
import jax.numpy as jnp
from jax import lax
from jax.experimental import pallas as pl
from jax.experimental.pallas import tpu as pltpu
from jax.sharding import PartitionSpec as P

AXES = ("wide", "narrow")
QUBITS = 7
FRONT_ROWS = 64
LAST_ROWS = 64
GATE_STEPS = 4
BACK_STEPS = 4
GATE = 128
f32 = jnp.float32
bf16 = jnp.bfloat16
VMEM = pl.BlockSpec(memory_space=pltpu.VMEM)
SMEM = pl.BlockSpec(memory_space=pltpu.SMEM)
ANY = pl.BlockSpec(memory_space=pl.ANY)
DMA = pltpu.SemaphoreType.DMA


def halves(value):
    high = value.astype(bf16)
    return high, (value - high.astype(f32)).astype(bf16)


def mul(left, right):
    return jnp.dot(left, right, preferred_element_type=f32)


def pick(states, orders_ref, row):
    mapped = jnp.zeros_like(states)
    for place in range(QUBITS):
        mapped = mapped + (((states >> place) & 1) << orders_ref[row, place])
    return (mapped == lax.broadcasted_iota(jnp.int32, (GATE, GATE), 1)).astype(bf16)


def turned(left, right):
    return lax.dot_general(left, right, (((1,), (1,)), ((), ())), preferred_element_type=f32)


def chosen(one_hot, gate):
    return [turned(turned(one_hot, part).astype(bf16), one_hot).astype(bf16) for part in halves(gate)]


def unit_turn(quarters):
    whole = jnp.floor(quarters + 0.5)
    r = (quarters - whole) * 1.5707963267948966
    s = r * r
    sine = r + r * s * (-1.6666654611e-1 + s * (8.3321608736e-3 - s * 1.9515295891e-4))
    cosine = 1.0 - 0.5 * s + s * s * (
        4.166664568298827e-2 + s * (-1.388731625493765e-3 + s * 2.443315711809948e-5)
    )
    quarter = whole.astype(jnp.int32)
    swap = (quarter & 1) == 1
    base_sin = jnp.where(swap, cosine, sine)
    base_cos = jnp.where(swap, sine, cosine)
    sine = jnp.where((quarter & 2) == 2, -base_sin, base_sin)
    cosine = jnp.where(((quarter + 1) & 2) == 2, -base_cos, base_cos)
    return cosine, sine


def moves(pairs, sems):
    return [pltpu.make_async_copy(a, b, sems.at[i]) for i, (a, b) in enumerate(pairs)]


def front_kernel(base_ref, orders_ref, masks_ref, angles_ref, real_ref, imag_ref, gates_ref,
                 send_ref, gate_ref, need_ref, weight_ref, table_ref, place_ref,
                 in_ref, out_ref, in_sems, out_sems):
    top, total = real_ref.shape[:2]
    count = FRONT_ROWS
    chunks = total // count
    pairs = masks_ref.shape[1]
    patterns = 2**pairs
    rows = top * count
    order = range(top)
    spans = [pl.ds(chunk * count, count) for chunk in range(chunks)]
    arrive = moves(
        [
            (ref.at[:, span], in_ref.at[part, :, span])
            for span in spans
            for part, ref in enumerate((real_ref, imag_ref))
        ],
        in_sems,
    )
    leave = moves([(out_ref.at[span], send_ref.at[span]) for span in spans], out_sems)
    for copy in arrive:
        copy.start()

    states = lax.broadcasted_iota(jnp.int32, (GATE, GATE), 0)
    one_hot = pick(states, orders_ref, 0)
    real_high, real_low = chosen(one_hot, gates_ref[0, 0])
    imag_high, imag_low = chosen(one_hot, gates_ref[0, 1])
    for spot, real, imag in (
        (0, real_high, imag_high),
        (2, real_low, imag_low),
        (4, real_high, imag_high),
    ):
        upper = slice(spot * GATE, (spot + 1) * GATE)
        lower = slice((spot + 1) * GATE, (spot + 2) * GATE)
        gate_ref[upper, :GATE] = real
        gate_ref[lower, :GATE] = -imag
        gate_ref[upper, GATE:] = imag
        gate_ref[lower, GATE:] = real
    lane = lax.broadcasted_iota(jnp.int32, (8, GATE), 1)
    spot = lax.broadcasted_iota(jnp.int32, (GATE, GATE), 0)
    column = lax.broadcasted_iota(jnp.int32, (patterns, GATE), 1)
    pattern = lax.broadcasted_iota(jnp.int32, (patterns, GATE), 0)
    need = jnp.zeros((8, GATE), jnp.int32) - 1
    weight = jnp.zeros((GATE, GATE), f32)
    quarters = jnp.zeros((patterns, GATE), f32)
    for pair in range(pairs):
        mask = masks_ref[0, pair] | masks_ref[1, pair]
        inside = mask & (GATE - 1)
        need = jnp.where(lane == pair, mask & ~(GATE - 1), need)
        weight = jnp.where(spot == pair, float(2**pair), weight)
        met = ((column & inside) == inside) & (((pattern >> pair) & 1) == 1)
        quarters = quarters + jnp.where(met, angles_ref[pair] * 0.6366197723675814, 0.0)
    need_ref[...] = need
    weight_ref[...] = weight.astype(bf16)
    for half, value in enumerate(unit_turn(quarters)):
        lanes = slice(half * GATE, (half + 1) * GATE)
        table_ref[:patterns, lanes], table_ref[patterns:, lanes] = halves(value)
    within = lax.broadcasted_iota(jnp.int32, (count, GATE), 0) * GATE
    for spot, high in enumerate(order):
        place_ref[spot] = within + (base_ref[0] + high * (256 * GATE))

    need = need_ref[0:1, :]
    lane = lax.broadcasted_iota(jnp.int32, (rows, GATE), 1).astype(f32)
    for chunk in range(chunks):
        span = slice(chunk * count, (chunk + 1) * count)
        arrive[2 * chunk].wait()
        arrive[2 * chunk + 1].wait()
        both = jnp.concatenate(
            [in_ref[part, :, span].reshape(rows, GATE) for part in range(2)], axis=1
        )
        x_high, x_low = halves(both)
        new = mul(jnp.concatenate([x_high, x_high, x_low], axis=1), gate_ref[...])
        flat = place_ref[...].reshape(rows, GATE) + chunk * (count * GATE)
        conditions = jnp.where((flat & need) == need, 1.0, 0.0).astype(bf16)
        found = mul(conditions, weight_ref[...])
        chosen_rows = [
            jnp.where(found == lane + float(first), 1.0, 0.0).astype(bf16)
            for first in range(0, patterns, GATE)
        ]
        turn = mul(jnp.concatenate(chosen_rows * 2, axis=1), table_ref[...])
        cosine, sine = turn[:, :GATE], turn[:, GATE:]
        real = new[:, :GATE]
        imag = new[:, GATE:]
        for part, value in enumerate((real * cosine - imag * sine, real * sine + imag * cosine)):
            out_ref[span, part] = jnp.transpose(value.reshape(top, count, GATE), (1, 0, 2))
        leave[chunk].start()
    for copy in leave:
        copy.wait()


def middle_kernel(second_ref, third_ref, got_ref, back_ref, gates_ref, mid_ref,
                  in_ref, out_ref, in_sems, out_sems):
    inputs, outputs = got_ref.shape[:2]
    apart = outputs // GATE_STEPS
    wide_apart = inputs // BACK_STEPS
    spans = [pl.ds(chunk * apart, apart) for chunk in range(GATE_STEPS)]
    arrive = moves([(got_ref.at[:, span], in_ref.at[:, span]) for span in spans], in_sems)
    spans = [pl.ds(chunk * wide_apart, wide_apart) for chunk in range(BACK_STEPS)]
    leave = moves([(out_ref.at[span], back_ref.at[span]) for span in spans], out_sems)
    for copy in arrive:
        copy.start()
    for which, ref in enumerate((second_ref, third_ref)):
        high, low = halves(ref[...])
        gates_ref[which] = jnp.concatenate([high, low], axis=0)

    def apply(which, x):
        x_high, x_low = halves(x)
        first = mul(gates_ref[which], x_high)
        return first[:256] + first[256:] + mul(gates_ref[which, :256], x_low)

    for narrow in range(outputs):
        if narrow % apart == 0:
            arrive[narrow // apart].wait()
        parts = [jnp.transpose(in_ref[:, narrow, part], (1, 0, 2)) for part in range(2)]
        columns = [
            jnp.concatenate([part[inner * 4 + rest] for part in parts for inner in range(4)], axis=0)
            for rest in range(4)
        ]
        out = apply(0, jnp.concatenate(columns, axis=1))
        for part in range(2):
            stack = jnp.stack(
                [
                    out[
                        part * GATE + inner * inputs : part * GATE + (inner + 1) * inputs,
                        rest * GATE : (rest + 1) * GATE,
                    ]
                    for rest in range(4)
                    for inner in range(4)
                ],
                axis=0,
            )
            mid_ref[part, :, narrow] = jnp.transpose(stack, (1, 0, 2))
    for group in range(inputs // 4):
        first = group * 4
        columns = [
            jnp.concatenate(
                [mid_ref[part, first + wide].reshape(GATE, GATE) for part in range(2)], axis=0
            )
            for wide in range(4)
        ]
        out = apply(1, jnp.concatenate(columns, axis=1))
        for wide in range(4):
            out_ref[first + wide] = out[:, wide * GATE : (wide + 1) * GATE].reshape(
                outputs, 2, 16, GATE
            )
        if (first + 4) % wide_apart == 0:
            leave[first // wide_apart].start()
    for copy in leave:
        copy.wait()


def last_kernel(got_ref, real_ref, imag_ref, in_ref, out_ref, in_sems, out_sems):
    chunks = got_ref.shape[0] // LAST_ROWS
    spans = [pl.ds(chunk * LAST_ROWS, LAST_ROWS) for chunk in range(chunks)]
    arrive = moves([(got_ref.at[span], in_ref.at[span]) for span in spans], in_sems)
    leave = moves(
        [
            (out_ref.at[part, :, span], ref.at[:, span])
            for span in spans
            for part, ref in enumerate((real_ref, imag_ref))
        ],
        out_sems,
    )
    for copy in arrive:
        copy.start()
    for chunk in range(chunks):
        span = slice(chunk * LAST_ROWS, (chunk + 1) * LAST_ROWS)
        arrive[chunk].wait()
        for part in range(2):
            out_ref[part, :, span] = jnp.transpose(in_ref[span, part], (1, 0, 2))
            leave[2 * chunk + part].start()
    for copy in leave:
        copy.wait()


def ordered(gate_pair, order_row, row_states, column_states):
    def one_hot(states):
        places = jnp.arange(QUBITS, dtype=jnp.int32)
        digits = states[:, None] >> places[None, :] & 1
        mapped = jnp.sum(digits << order_row[None, :], axis=1)
        return (mapped[:, None] == jnp.arange(GATE, dtype=jnp.int32)[None, :]).astype(f32)

    precise = lax.Precision.HIGHEST
    left, right = one_hot(row_states), one_hot(column_states)
    return [
        jnp.dot(jnp.dot(left, part, precision=precise), right.T, precision=precise)
        for part in (gate_pair[0], gate_pair[1])
    ]


def body(state_real, state_imag, gates, gate_orders, phase_masks, phase_angles):
    real_part = state_real[0, 0]
    imag_part = state_imag[0, 0]
    rows, columns = real_part.shape
    wide_count = lax.axis_size("wide")
    narrow_count = lax.axis_size("narrow")
    devices = wide_count * narrow_count
    base = (lax.axis_index("narrow") * wide_count + lax.axis_index("wide")) * (rows * columns)
    packed = jax.ShapeDtypeStruct((devices, 2, 16, columns), f32)
    tall = jax.ShapeDtypeStruct((16, devices, columns), f32)
    count = FRONT_ROWS
    send = pl.pallas_call(
        front_kernel,
        out_shape=packed,
        in_specs=[SMEM] * 4 + [ANY, ANY, VMEM],
        out_specs=ANY,
        scratch_shapes=[
            pltpu.VMEM((768, 256), bf16),
            pltpu.VMEM((8, GATE), jnp.int32),
            pltpu.VMEM((GATE, GATE), bf16),
            pltpu.VMEM((2 * 2 ** phase_masks.shape[0], 256), bf16),
            pltpu.VMEM((16, count, GATE), jnp.int32),
            pltpu.VMEM((2, 16, devices, columns), f32),
            pltpu.VMEM((devices, 2, 16, columns), f32),
            DMA((2 * devices // count,)),
            DMA((devices // count,)),
        ],
        name="front",
    )(
        base[None],
        gate_orders,
        phase_masks.T,
        phase_angles,
        real_part.reshape(16, devices, columns),
        imag_part.reshape(16, devices, columns),
        gates,
    )

    def exchange(block):
        return lax.all_to_all(block, AXES, split_axis=0, concat_axis=0, tiled=True)

    got = exchange(send)
    states = jnp.arange(GATE, dtype=jnp.int32)
    by_inner = states % 32 * 4 + states // 32
    second = ordered(gates[1], gate_orders[1], by_inner, by_inner)
    swapped = states // 16 * 16 + states % 4 * 4 + states // 4 % 4
    third = ordered(gates[2], gate_orders[2], states, swapped)
    second = jnp.concatenate(
        [
            jnp.concatenate([second[0], -second[1]], axis=1),
            jnp.concatenate([second[1], second[0]], axis=1),
        ],
        axis=0,
    )
    third = jnp.stack(
        [
            jnp.concatenate([third[0], -third[1]], axis=1).reshape(8, 16, 256),
            jnp.concatenate([third[1], third[0]], axis=1).reshape(8, 16, 256),
        ],
        axis=1,
    ).reshape(256, 256)
    back = pl.pallas_call(
        middle_kernel,
        out_shape=jax.ShapeDtypeStruct((wide_count, narrow_count, 2, 16, columns), f32),
        in_specs=[VMEM, VMEM, ANY],
        out_specs=ANY,
        scratch_shapes=[
            pltpu.VMEM((2, 512, 256), bf16),
            pltpu.VMEM((2, wide_count, narrow_count, 16, columns), f32),
            pltpu.VMEM((wide_count, narrow_count, 2, 16, columns), f32),
            pltpu.VMEM((wide_count, narrow_count, 2, 16, columns), f32),
            DMA((GATE_STEPS,)),
            DMA((BACK_STEPS,)),
        ],
        name="middle",
    )(second, third, got.reshape(wide_count, narrow_count, 2, 16, columns))
    final = exchange(back.reshape(devices, 2, 16, columns))
    out_real, out_imag = pl.pallas_call(
        last_kernel,
        out_shape=(tall, tall),
        in_specs=[ANY],
        out_specs=(ANY, ANY),
        scratch_shapes=[
            pltpu.VMEM((devices, 2, 16, columns), f32),
            pltpu.VMEM((2, 16, devices, columns), f32),
            DMA((devices // LAST_ROWS,)),
            DMA((2 * devices // LAST_ROWS,)),
        ],
        name="last",
    )(final)
    out_real, out_imag = out_real.reshape(rows, columns), out_imag.reshape(rows, columns)
    return (out_real[None, None], out_imag[None, None])


def solution(mesh):
    placed = (P("narrow", "wide", None, None), P("narrow", "wide", None, None), P(), P(), P(), P())
    return jax.shard_map(
        body,
        mesh=mesh,
        in_specs=placed,
        out_specs=(P("narrow", "wide", None, None), P("narrow", "wide", None, None)),
        check_vma=False,
    )
```

time: 248 us -> 240 us (0.968)
  Pallas kernels: 26.4 us -> 19.6 us
    pallas_call x1, Pallas kernels: 12.5 us -> 8.17 us  [body(): pl.pallas_call(middle_kernel, out_shape=jax.ShapeDtypeStruct((wide_count,...]
where the time goes in v6:
time: 240 us; the launch traced here: 238 us
  blocking collectives  106 us (44%)
  waiting for transfers between devices  92.4 us (38%)
  Pallas kernels  19.6 us (8%)
  starting transfers between devices  15.7 us (7%)
    all_to_all x1, blocking collectives, exchange(): return lax.all_to_all(block, AXES, split_axis=0, concat_axis=0, tiled=True)  106 us
    all_to_all x1, waiting for transfers between devices, exchange(): return lax.all_to_all(block, AXES, split_axis=0, concat_axis=0, tiled=True)  92.4 us
    all_to_all x1, starting transfers between devices, exchange(): return lax.all_to_all(block, AXES, split_axis=0, concat_axis=0, tiled=True)  15.7 us
    pallas_call x1, Pallas kernels, body(): pl.pallas_call(middle_kernel, out_shape=jax.ShapeDtypeStruct((wide_count,...  8.17 us
    pallas_call x1, Pallas kernels, body(): pl.pallas_call(front_kernel, out_shape=packed, in_specs=[SMEM] * 4 + [ANY...  8.01 us
  transfers between devices with their start and end apart: 1, of which 1 were waited for; matrix products, arithmetic and copies ran while one was open for 2% of the time, Pallas kernels for 0%

profile of v6, /device:TPU:2, one launch (start us, length us, event | category | flops | bytes accessed | tf_op | source)
XLA Modules:
  0.0 238.0 jit_solution(15236649197652489435)
XLA Ops:
  0.6 8.0 %front.1 = f32[256,2,16,128]{3,2,1,0:T(8,128)} custom-call(s32[1]{0:T(128)} %bitcast.9.base_ref, s32[3,7]{1,0:T(4,128)} %orders_ref.1, s32[2,8]{1,0:T(2,128)} %bitcast.37, f32[8]{0:T(128)} %angles_ref.1, f32[16,256,128]{2,1,0:T(8,128)} %bitcast.32, f32[16,256,128]{2,1,0:T(8,128)} %bitcast.33, f32[3,2,128,128]{3,2,1,0:T(8,128)} %gates_ref.1), custom_call_target="tpu_custom_call" | custom-call | tf_op jit(solution)/shard_map/front/pallas_call | solution.py:271
  8.7 0.0 copy-start.1
  8.7 0.0 copy-start
  8.7 15.7 %all-to-all-start = ((f32[256,2,16,128]{3,2,1,0:T(8,128)}), f32[256,2,16,128]{3,2,1,0:T(8,128)}, u32[]{:S(2)}, u32[]{:S(2)}) async-start(f32[256,2,16,128]{3,2,1,0:T(8,128)} %front.1), calls=%async_computation | async-start | bytes 8388608 | tf_op jit(solution)/shard_map/all_to_all | solution.py:299
  24.4 0.0 copy-done.1
  24.4 0.1 shift-left_reduce_fusion
  24.5 0.0 copy-done
  24.5 0.2 fusion
  24.8 0.2 fusion.2
  25.0 0.2 fusion.10
  25.2 0.2 fusion.33
  25.5 0.1 copy.25
  25.6 0.1 copy.26
  25.8 0.7 copy.27
  26.5 0.2 fusion.4
  26.7 0.2 fusion.6
  26.9 0.3 fusion.15
  27.2 0.3 fusion.32
  27.5 0.7 maximum_maximum_fusion.second_ref
  28.2 92.4 %all-to-all-done = f32[256,2,16,128]{3,2,1,0:T(8,128)} async-done(((f32[256,2,16,128]{3,2,1,0:T(8,128)}), f32[256,2,16,128]{3,2,1,0:T(8,128)}, u32[]{:S(2)}, u32[]{:S(2)}) %all-to-all-start) | async-done | bytes 4194336 | tf_op jit(solution)/shard_map/all_to_all | solution.py:299
  120.7 8.2 %middle.1 = f32[32,8,2,16,128]{4,3,2,1,0:T(8,128)} custom-call(f32[256,256]{1,0:T(8,128)} %maximum_maximum_fusion.second_ref, f32[256,256]{1,0:T(8,128)} %bitcast.34, f32[32,8,2,16,128]{4,3,2,1,0:T(8,128)} %bitcast.13.got_ref), custom_call_target="tpu_custom_call" | custom-call | tf_op jit(solution)/shard_map/middle/pallas_call | solution.py:321
  128.9 105.5 %all_to_all.10.got_ref = f32[256,2,16,128]{3,2,1,0:T(8,128)} all-to-all(f32[256,2,16,128]{3,2,1,0:T(8,128)} %bitcast.31), channel_id=1, replica_groups=mesh['wide'=32,'narrow'=8] {'wide','narrow'}, dimensions={0} | all-to-all | bytes 8388608 | tf_op jit(solution)/shard_map/all_to_all | solution.py:299
  234.4 3.5 %last.1 = (f32[16,256,128]{2,1,0:T(8,128)}, f32[16,256,128]{2,1,0:T(8,128)}) custom-call(f32[256,2,16,128]{3,2,1,0:T(8,128)} %all_to_all.10.got_ref), custom_call_target="tpu_custom_call" | custom-call | tf_op jit(solution)/shard_map/last/pallas_call | solution.py:337
  (5 shorter events, 0.1 us)
Async XLA Ops:
  8.7 15.7 %copy-start.1 = (s32[3,7]{1,0:T(4,128)S(1)}, s32[3,7]{1,0:T(4,128)}, u32[]{:S(2)}) copy-start(s32[3,7]{1,0:T(4,128)} %orders_ref.1) | copy-start | bytes 256
  8.7 15.8 %copy-start = (f32[3,2,128,128]{3,2,1,0:T(8,128)S(1)}, f32[3,2,128,128]{3,2,1,0:T(8,128)}, u32[]{:S(2)}) copy-start(f32[3,2,128,128]{3,2,1,0:T(8,128)} %gates_ref.1) | copy-start | bytes 1179652
  8.7 112.0 %all-to-all-start = ((f32[256,2,16,128]{3,2,1,0:T(8,128)}), f32[256,2,16,128]{3,2,1,0:T(8,128)}, u32[]{:S(2)}, u32[]{:S(2)}) async-start(f32[256,2,16,128]{3,2,1,0:T(8,128)} %front.1), calls=%async_computation | async-start | bytes 8388608 | tf_op jit(solution)/shard_map/all_to_all | solution.py:299

commit v7 on v6

--- a/solution.py
+++ b/solution.py
@@ -11,8 +11,7 @@
 QUBITS = 7
 FRONT_ROWS = 64
 LAST_ROWS = 64
-GATE_STEPS = 4
-BACK_STEPS = 4
+GATE_STEPS = 2
 GATE = 128
 f32 = jnp.float32
 bf16 = jnp.bfloat16
@@ -157,65 +156,63 @@
         copy.wait()
 
 
-def middle_kernel(second_ref, third_ref, got_ref, back_ref, gates_ref, mid_ref,
-                  in_ref, out_ref, in_sems, out_sems):
-    inputs, outputs = got_ref.shape[:2]
-    apart = outputs // GATE_STEPS
-    wide_apart = inputs // BACK_STEPS
-    spans = [pl.ds(chunk * apart, apart) for chunk in range(GATE_STEPS)]
-    arrive = moves([(got_ref.at[:, span], in_ref.at[:, span]) for span in spans], in_sems)
-    spans = [pl.ds(chunk * wide_apart, wide_apart) for chunk in range(BACK_STEPS)]
-    leave = moves([(out_ref.at[span], back_ref.at[span]) for span in spans], out_sems)
-    for copy in arrive:
-        copy.start()
-    for which, ref in enumerate((second_ref, third_ref)):
-        high, low = halves(ref[...])
-        gates_ref[which] = jnp.concatenate([high, low], axis=0)
+def middle_kernel(second_ref, third_ref, got_ref, back_ref, mid_ref, gates_ref):
+    step = pl.program_id(0)
+    inputs, together = got_ref.shape[:2]
+    steps = 8 // together
+
+    @pl.when(step == 0)
+    def _():
+        for which, ref in enumerate((second_ref, third_ref)):
+            high, low = halves(ref[...])
+            gates_ref[which] = jnp.concatenate([high, low, high], axis=1)
 
     def apply(which, x):
         x_high, x_low = halves(x)
-        first = mul(gates_ref[which], x_high)
-        return first[:256] + first[256:] + mul(gates_ref[which, :256], x_low)
-
-    for narrow in range(outputs):
-        if narrow % apart == 0:
-            arrive[narrow // apart].wait()
-        parts = [jnp.transpose(in_ref[:, narrow, part], (1, 0, 2)) for part in range(2)]
-        columns = [
-            jnp.concatenate([part[inner * 4 + rest] for part in parts for inner in range(4)], axis=0)
-            for rest in range(4)
-        ]
-        out = apply(0, jnp.concatenate(columns, axis=1))
-        for part in range(2):
-            stack = jnp.stack(
-                [
-                    out[
-                        part * GATE + inner * inputs : part * GATE + (inner + 1) * inputs,
-                        rest * GATE : (rest + 1) * GATE,
-                    ]
-                    for rest in range(4)
-                    for inner in range(4)
-                ],
-                axis=0,
-            )
-            mid_ref[part, :, narrow] = jnp.transpose(stack, (1, 0, 2))
-    for group in range(inputs // 4):
-        first = group * 4
-        columns = [
-            jnp.concatenate(
-                [mid_ref[part, first + wide].reshape(GATE, GATE) for part in range(2)], axis=0
-            )
-            for wide in range(4)
-        ]
-        out = apply(1, jnp.concatenate(columns, axis=1))
-        for wide in range(4):
-            out_ref[first + wide] = out[:, wide * GATE : (wide + 1) * GATE].reshape(
-                outputs, 2, 16, GATE
-            )
-        if (first + 4) % wide_apart == 0:
-            leave[first // wide_apart].start()
-    for copy in leave:
-        copy.wait()
+        return mul(gates_ref[which], jnp.concatenate([x_high, x_high, x_low], axis=0))
+
+    @pl.when(step < steps)
+    def _():
+        for narrow in range(together):
+            parts = [jnp.transpose(got_ref[:, narrow, part], (1, 0, 2)) for part in range(2)]
+            columns = [
+                jnp.concatenate(
+                    [part[inner * 4 + rest] for part in parts for inner in range(4)], axis=0
+                )
+                for rest in range(4)
+            ]
+            out = apply(0, jnp.concatenate(columns, axis=1))
+            for part in range(2):
+                stack = jnp.stack(
+                    [
+                        out[
+                            part * GATE + inner * inputs : part * GATE + (inner + 1) * inputs,
+                            rest * GATE : (rest + 1) * GATE,
+                        ]
+                        for rest in range(4)
+                        for inner in range(4)
+                    ],
+                    axis=0,
+                )
+                mid_ref[part, :, step * together + narrow] = jnp.transpose(stack, (1, 0, 2))
+
+    @pl.when(step >= steps)
+    def _():
+        count = back_ref.shape[0]
+
+        for group in range(count // 4):
+            first = (step - steps) * count + group * 4
+            columns = [
+                jnp.concatenate(
+                    [mid_ref[part, first + wide].reshape(GATE, GATE) for part in range(2)], axis=0
+                )
+                for wide in range(4)
+            ]
+            out = apply(1, jnp.concatenate(columns, axis=1))
+            for wide in range(4):
+                back_ref[group * 4 + wide] = out[:, wide * GATE : (wide + 1) * GATE].reshape(
+                    8, 2, 16, GATE
+                )
 
 
 def last_kernel(got_ref, real_ref, imag_ref, in_ref, out_ref, in_sems, out_sems):
@@ -321,15 +318,22 @@
     back = pl.pallas_call(
         middle_kernel,
         out_shape=jax.ShapeDtypeStruct((wide_count, narrow_count, 2, 16, columns), f32),
-        in_specs=[VMEM, VMEM, ANY],
-        out_specs=ANY,
+        grid=(GATE_STEPS * 2,),
+        in_specs=[
+            VMEM,
+            VMEM,
+            pl.BlockSpec(
+                (wide_count, narrow_count // GATE_STEPS, 2, 16, columns),
+                lambda i: (0, jnp.minimum(i, GATE_STEPS - 1), 0, 0, 0),
+            ),
+        ],
+        out_specs=pl.BlockSpec(
+            (wide_count // GATE_STEPS, narrow_count, 2, 16, columns),
+            lambda i: (jnp.maximum(i - GATE_STEPS, 0), 0, 0, 0, 0),
+        ),
         scratch_shapes=[
-            pltpu.VMEM((2, 512, 256), bf16),
             pltpu.VMEM((2, wide_count, narrow_count, 16, columns), f32),
-            pltpu.VMEM((wide_count, narrow_count, 2, 16, columns), f32),
-            pltpu.VMEM((wide_count, narrow_count, 2, 16, columns), f32),
-            DMA((GATE_STEPS,)),
-            DMA((BACK_STEPS,)),
+            pltpu.VMEM((2, 256, 768), bf16),
         ],
         name="middle",
     )(second, third, got.reshape(wide_count, narrow_count, 2, 16, columns))

time: 240 us -> 240 us (level)
  no operation moved by 1% of the time
where the time goes in v7:
time: 240 us; the launch traced here: 238 us
  blocking collectives  105 us (44%)
  waiting for transfers between devices  92.4 us (38%)
  Pallas kernels  19.5 us (8%)
  starting transfers between devices  15.7 us (7%)
    all_to_all x1, blocking collectives, exchange(): return lax.all_to_all(block, AXES, split_axis=0, concat_axis=0, tiled=True)  105 us
    all_to_all x1, waiting for transfers between devices, exchange(): return lax.all_to_all(block, AXES, split_axis=0, concat_axis=0, tiled=True)  92.4 us
    all_to_all x1, starting transfers between devices, exchange(): return lax.all_to_all(block, AXES, split_axis=0, concat_axis=0, tiled=True)  15.7 us
    pallas_call x1, Pallas kernels, body(): pl.pallas_call(middle_kernel, out_shape=jax.ShapeDtypeStruct((wide_count,...  8.07 us
    pallas_call x1, Pallas kernels, body(): pl.pallas_call(front_kernel, out_shape=packed, in_specs=[SMEM] * 4 + [ANY...  8 us
  transfers between devices with their start and end apart: 1, of which 1 were waited for; matrix products, arithmetic and copies ran while one was open for 2% of the time, Pallas kernels for 0%

profile of v7, /device:TPU:2, one launch (start us, length us, event | category | flops | bytes accessed | tf_op | source)
XLA Modules:
  0.0 237.6 jit_solution(6749705673010528457)
XLA Ops:
  0.6 8.0 %front.1 = f32[256,2,16,128]{3,2,1,0:T(8,128)} custom-call(s32[1]{0:T(128)} %bitcast.9.base_ref, s32[3,7]{1,0:T(4,128)} %orders_ref.1, s32[2,8]{1,0:T(2,128)} %bitcast.37, f32[8]{0:T(128)} %angles_ref.1, f32[16,256,128]{2,1,0:T(8,128)} %bitcast.32, f32[16,256,128]{2,1,0:T(8,128)} %bitcast.33, f32[3,2,128,128]{3,2,1,0:T(8,128)} %gates_ref.1), custom_call_target="tpu_custom_call" | custom-call | tf_op jit(solution)/shard_map/front/pallas_call | solution.py:268
  8.6 0.0 copy-start.1
  8.7 0.0 copy-start
  8.7 15.7 %all-to-all-start = ((f32[256,2,16,128]{3,2,1,0:T(8,128)}), f32[256,2,16,128]{3,2,1,0:T(8,128)}, u32[]{:S(2)}, u32[]{:S(2)}) async-start(f32[256,2,16,128]{3,2,1,0:T(8,128)} %front.1), calls=%async_computation | async-start | bytes 8388608 | tf_op jit(solution)/shard_map/all_to_all | solution.py:296
  24.4 0.0 copy-done.1
  24.4 0.1 shift-left_reduce_fusion
  24.5 0.0 copy-done
  24.5 0.2 fusion
  24.8 0.2 fusion.2
  25.0 0.2 fusion.10
  25.2 0.2 fusion.33
  25.5 0.1 copy.25
  25.6 0.1 copy.26
  25.8 0.7 copy.27
  26.5 0.2 fusion.4
  26.7 0.2 fusion.6
  27.0 0.3 fusion.15
  27.2 0.3 fusion.32
  27.5 0.7 maximum_maximum_fusion.second_ref
  28.2 92.4 %all-to-all-done = f32[256,2,16,128]{3,2,1,0:T(8,128)} async-done(((f32[256,2,16,128]{3,2,1,0:T(8,128)}), f32[256,2,16,128]{3,2,1,0:T(8,128)}, u32[]{:S(2)}, u32[]{:S(2)}) %all-to-all-start) | async-done | bytes 4194336 | tf_op jit(solution)/shard_map/all_to_all | solution.py:296
  120.7 8.1 %middle.1 = f32[32,8,2,16,128]{4,3,2,1,0:T(8,128)} custom-call(f32[256,256]{1,0:T(8,128)} %maximum_maximum_fusion.second_ref, f32[256,256]{1,0:T(8,128)} %bitcast.34, f32[32,8,2,16,128]{4,3,2,1,0:T(8,128)} %bitcast.13.got_ref), custom_call_target="tpu_custom_call" | custom-call | tf_op jit(solution)/shard_map/middle/pallas_call | solution.py:318
  128.8 105.3 %all_to_all.10.got_ref = f32[256,2,16,128]{3,2,1,0:T(8,128)} all-to-all(f32[256,2,16,128]{3,2,1,0:T(8,128)} %bitcast.31), channel_id=1, replica_groups=mesh['wide'=32,'narrow'=8] {'wide','narrow'}, dimensions={0} | all-to-all | bytes 8388608 | tf_op jit(solution)/shard_map/all_to_all | solution.py:296
  234.1 3.5 %last.1 = (f32[16,256,128]{2,1,0:T(8,128)}, f32[16,256,128]{2,1,0:T(8,128)}) custom-call(f32[256,2,16,128]{3,2,1,0:T(8,128)} %all_to_all.10.got_ref), custom_call_target="tpu_custom_call" | custom-call | tf_op jit(solution)/shard_map/last/pallas_call | solution.py:341
  (5 shorter events, 0.1 us)
Async XLA Ops:
  8.6 15.8 %copy-start.1 = (s32[3,7]{1,0:T(4,128)S(1)}, s32[3,7]{1,0:T(4,128)}, u32[]{:S(2)}) copy-start(s32[3,7]{1,0:T(4,128)} %orders_ref.1) | copy-start | bytes 256
  8.7 15.9 %copy-start = (f32[3,2,128,128]{3,2,1,0:T(8,128)S(1)}, f32[3,2,128,128]{3,2,1,0:T(8,128)}, u32[]{:S(2)}) copy-start(f32[3,2,128,128]{3,2,1,0:T(8,128)} %gates_ref.1) | copy-start | bytes 1179652
  8.7 112.0 %all-to-all-start = ((f32[256,2,16,128]{3,2,1,0:T(8,128)}), f32[256,2,16,128]{3,2,1,0:T(8,128)}, u32[]{:S(2)}, u32[]{:S(2)}) async-start(f32[256,2,16,128]{3,2,1,0:T(8,128)} %front.1), calls=%async_computation | async-start | bytes 8388608 | tf_op jit(solution)/shard_map/all_to_all | solution.py:296
